TPU v7x, 256 devices: a whole 4x4x8 slice. The times are simulated.
256 devices in a mesh: section: 32 (over z_lo, y, core), tensor: 8 (over z_hi, x).
Axes of the slice: x: 4, y: 4, z: 8 (z_hi: 2, z_lo: 4; z = z_hi * 4 + z_lo), core: 2. Of those that a mesh axis runs over, the one named last changes fastest.
Arguments:
- queries: bfloat16 [8192, 4096], P('section', 'tensor'), may hold values from -180 to 180
- memory: bfloat16 [512, 4096], P('section', 'tensor'), may hold values from -6 to 6
- key_weight: bfloat16 [65536, 4096], P('section', 'tensor'), may hold values from -0.09375 to 0.09375
- value_weight: bfloat16 [65536, 4096], P('section', 'tensor'), may hold values from -0.09375 to 0.09375
- grad_context: bfloat16 [8192, 4096], P('section', 'tensor'), may hold values from -6 to 6
- memory_lengths: int32 [4], replicated, may hold values from 64 to 128, as said below
Outputs:
- context: bfloat16 [8192, 4096], P('section', 'tensor')
- grad_queries: bfloat16 [8192, 4096], P('section', 'tensor')
- grad_memory: float32 [512, 4096], P('section', 'tensor')
Inputs may be any that keep to these rules, and one draw needn't show every extreme that they name: `memory_lengths`: one reaction in every draw has all 128 encoder tokens.
All inputs are finite; a program needn't handle non-finite values.
Results may differ from a plain program's by a relative error of at most 0.0171.
The roundings to bfloat16 on the way count: a program that leaves them out, or rounds other values in their place, can miss the bound.
Values may be sent and summed in bfloat16 or wider, within the bound.
No kernel may reach another device: no remote copies, remote signals or barrier semaphores. Data moves between devices by JAX's collectives and lax.ppermute only.
A program may use at most 64 MiB of HBM per device.

v0:
```python
import jax
import jax.numpy as jnp
from jax import lax
from jax.sharding import PartitionSpec as P

HDIM = 64


def partner(block, axis, distance):
    count = lax.axis_size(axis)
    route = []
    for low in range(count):
        high = low | 1 << distance
        if high != low and high < count:
            route += [(low, high), (high, low)]
    return lax.ppermute(block, axis, route)


def times_transposed(left, weight_rows):
    return lax.dot_general(
        left, weight_rows, (((1,), (1,)), ((), ())), preferred_element_type=jnp.float32
    )


def body(queries, memory, key_weight, value_weight, grad_context, memory_lengths):
    scale = HDIM ** (-0.5)
    parity = lax.axis_index("section") % 2
    react = memory_lengths.shape[0]
    half_react = react // 2
    head_cols = queries.shape[1]
    local_heads = head_cols // HDIM
    half_width = key_weight.shape[0]
    full_width = 2 * half_width
    half_start = parity * half_width
    full_rows = lax.all_gather(memory, "tensor", axis=1, tiled=True)
    own_cols = lax.dynamic_slice_in_dim(
        lax.all_gather(full_rows, "section", axis=0, tiled=True), half_start, half_width, 1
    )
    key_part = jnp.dot(own_cols, key_weight, preferred_element_type=jnp.float32)
    value_part = jnp.dot(own_cols, value_weight, preferred_element_type=jnp.float32)
    joined = jnp.concatenate([key_part, value_part], axis=1)
    key_all = joined[:, :head_cols]
    value_all = joined[:, head_cols:]
    half_rows = key_all.shape[0] // 2
    is_first = parity == 0
    own_key = jnp.where(is_first, key_all[:half_rows], key_all[half_rows:])
    other_key = jnp.where(is_first, key_all[half_rows:], key_all[:half_rows])
    own_value = jnp.where(is_first, value_all[:half_rows], value_all[half_rows:])
    other_value = jnp.where(is_first, value_all[half_rows:], value_all[:half_rows])
    recv_key, recv_value = partner((other_key, other_value), "section", 0)
    keys = (own_key + recv_key).astype(jnp.bfloat16)
    values = (own_value + recv_value).astype(jnp.bfloat16)
    lengths = lax.dynamic_slice_in_dim(memory_lengths, parity * half_react, half_react, 0)
    enc_len = keys.shape[0] // half_react
    dec_len = queries.shape[0] // half_react
    query_h = queries.reshape(half_react, dec_len, local_heads, HDIM)
    key_h = keys.reshape(half_react, enc_len, local_heads, HDIM)
    value_h = values.reshape(half_react, enc_len, local_heads, HDIM)
    cot_h = grad_context.reshape(half_react, dec_len, local_heads, HDIM)
    scores = (
        jnp.einsum("rqhd,rkhd->rhqk", query_h, key_h, preferred_element_type=jnp.float32) * scale
    )
    valid = jnp.arange(enc_len, dtype=jnp.int32)[None, :] < lengths[:, None]
    scores = jnp.where(valid[:, None, None, :], scores, jnp.float32(-1e30))
    top = jnp.max(scores, axis=-1, keepdims=True)
    expo = jnp.exp(scores - top)
    probs = expo / jnp.sum(expo, axis=-1, keepdims=True)
    probs_b = probs.astype(jnp.bfloat16)
    context = jnp.einsum(
        "rhqk,rkhd->rqhd", probs_b, value_h, preferred_element_type=jnp.float32
    ).astype(jnp.bfloat16)
    grad_p = jnp.einsum("rqhd,rkhd->rhqk", cot_h, value_h, preferred_element_type=jnp.float32)
    delta = jnp.sum(probs * grad_p, axis=-1, keepdims=True)
    grad_s = (probs * (grad_p - delta) * scale).astype(jnp.bfloat16)
    grad_q = jnp.einsum(
        "rhqk,rkhd->rqhd", grad_s, key_h, preferred_element_type=jnp.float32
    ).astype(jnp.bfloat16)
    key_grad = jnp.einsum(
        "rhqk,rqhd->rkhd", grad_s, query_h, preferred_element_type=jnp.float32
    ).astype(jnp.bfloat16)
    value_grad = jnp.einsum(
        "rhqk,rqhd->rkhd", probs_b, cot_h, preferred_element_type=jnp.float32
    ).astype(jnp.bfloat16)
    key_grad = key_grad.reshape(half_react * enc_len, head_cols)
    value_grad = value_grad.reshape(half_react * enc_len, head_cols)
    partner_key, partner_value = partner((key_grad, value_grad), "section", 0)
    layer_key_grad = jnp.where(
        is_first,
        jnp.concatenate([key_grad, partner_key], axis=0),
        jnp.concatenate([partner_key, key_grad], axis=0),
    )
    layer_value_grad = jnp.where(
        is_first,
        jnp.concatenate([value_grad, partner_value], axis=0),
        jnp.concatenate([partner_value, value_grad], axis=0),
    )
    block = times_transposed(layer_key_grad, key_weight) + times_transposed(
        layer_value_grad, value_weight
    )
    blank_rows = jnp.zeros((block.shape[0], full_width), jnp.float32)
    layer_total = lax.psum_scatter(
        lax.dynamic_update_slice_in_dim(blank_rows, block, half_start, 1),
        "section",
        scatter_dimension=0,
        tiled=True,
    )
    grad_memory = lax.psum_scatter(layer_total, "tensor", scatter_dimension=1, tiled=True)
    return (
        context.reshape(half_react * dec_len, head_cols),
        grad_q.reshape(half_react * dec_len, head_cols),
        grad_memory,
    )


def solution(mesh):
    placed = (
        P("section", "tensor"),
        P("section", "tensor"),
        P("section", "tensor"),
        P("section", "tensor"),
        P("section", "tensor"),
        P(),
    )
    return jax.shard_map(
        body,
        mesh=mesh,
        in_specs=placed,
        out_specs=(P("section", "tensor"), P("section", "tensor"), P("section", "tensor")),
        check_vma=False,
    )
```

profile of v0, /device:TPU:1, one launch (start us, length us, event | category | flops | bytes accessed | tf_op | source)
XLA Modules:
  0.0 409.7 jit_solution(8636467715947990893)
XLA Ops:
  7.2 42.8 %all_gather.6 = bf16[16,4096]{1,0:T(8,128)(2,1)} all-gather(bf16[16,512]{1,0:T(8,128)(2,1)} %param.7), channel_id=1, replica_groups=mesh['section'=32,'tensor'=8] {'tensor'}, dimensions={1}, use_global_device_ids=true | all-gather | bytes 147456 | tf_op jit(solution)/shard_map/all_gather | solution.py:35
  50.1 70.3 %all-gather.2.cloned.1.call-done = bf16[512,4096]{1,0:T(8,128)(2,1)} async-done(((bf16[16,4096]{1,0:T(8,128)(2,1)}), bf16[512,4096]{1,0:T(8,128)(2,1)}) %all-gather.2.cloned.1.call-update) | async-done | bytes 4194320 | tf_op jit(solution)/shard_map/all_gather | solution.py:37
  120.4 3.0 fusion.2
  123.4 1.0 slice_select_fusion
  124.7 1.2 fusion.4
  125.9 0.9 slice_select_fusion.1
  127.1 1.1 reshape.62
  128.1 2.0 copy.26
  130.2 2.1 reshape.63
  132.2 1.3 copy.33
  133.8 2.2 add_convert_fusion
  135.9 2.1 reshape.61
  138.0 2.0 copy.25
  140.0 1.9 add_convert_fusion.1
  141.9 1.3 reshape.60
  143.2 1.0 copy.28
  144.3 2.6 fusion.50
  146.9 0.8 fusion.17
  148.4 1.4 convolution_bitcast_fusion
  149.8 3.0 fusion.16
  152.8 1.2 copy.39
  154.0 0.5 collective-permute-start.2
  154.5 3.1 fusion.27
  157.6 4.2 %broadcast_in_dim.23 = f32[512,4096]{1,0:T(8,128)} broadcast(f32[]{:T(128)} %constant.34.clone.1), dimensions={} | broadcast | bytes 8388612 | tf_op jit(solution)/shard_map/broadcast_in_dim | solution.py:100
  161.9 3.3 add_dynamic-update-slice_fusion
  165.2 150.4 %reduce-scatter.3.cloned.1.call-done = f32[16,4096]{1,0:T(8,128)} async-done(((f32[512,4096]{1,0:T(8,128)}), f32[16,4096]{1,0:T(8,128)}) %reduce-scatter.3.cloned.1.call-update) | async-done | bytes 262160 | tf_op jit(solution)/shard_map/reduce_scatter | solution.py:101
  315.7 2.9 fusion.15
  318.6 1.2 copy.50
  319.9 1.0 reshape.59
  320.9 1.8 fusion.14
  323.0 1.0 reshape.58
  324.1 79.1 %reduce-scatter.5.cloned.1.call-done = f32[16,512]{1,0:T(8,128)} async-done(((f32[16,4096]{1,0:T(8,128)}), f32[16,512]{1,0:T(8,128)}) %reduce-scatter.5.cloned.1.call-update) | async-done | bytes 32784 | tf_op jit(solution)/shard_map/reduce_scatter | solution.py:107
  (39 shorter events, 1.9 us)
Async XLA Ops:
  7.2 113.2 %copy-start = (bf16[2048,512]{1,0:T(8,128)(2,1)S(1)}, bf16[2048,512]{1,0:T(8,128)(2,1)}, u32[]{:S(2)}) copy-start(bf16[2048,512]{1,0:T(8,128)(2,1)} %param.8) | copy-start | bytes 6291460
  7.2 113.2 %all-gather.2.cloned.1.call-start = ((), (), s32[]{:S(2)}) async-start(), calls=%async_computation.2 | async-start | bytes 4325376 | tf_op jit(solution)/shard_map/all_gather | solution.py:37
  50.0 265.7 %reduce-scatter.3.cloned.1.call-start = ((), (), s32[]{:S(2)}) async-start(), calls=%async_computation.3 | async-start | bytes 8650752 | tf_op jit(solution)/shard_map/reduce_scatter | solution.py:101
  120.4 4.3 %copy-start.2 = (bf16[2048,512]{1,0:T(8,128)(2,1)S(1)}, bf16[2048,512]{1,0:T(8,128)(2,1)}, u32[]{:S(2)}) copy-start(bf16[2048,512]{1,0:T(8,128)(2,1)} %param.9) | copy-start | bytes 6291460
  120.4 4.3 %copy-start.8 = (bf16[512,4096]{1,0:T(8,128)(2,1)S(1)}, bf16[512,4096]{1,0:T(8,128)(2,1)}, u32[]{:S(2)}) copy-start(bf16[512,4096]{1,0:T(8,128)(2,1)} %all-gather.2.cloned.1.call-done) | copy-start | bytes 12582916
  123.4 2.5 copy-start.1
  124.4 2.7 copy-start.4
  124.4 9.4 %collective-permute-start.1 = (f32[256,512]{1,0:T(8,128)}, f32[256,512]{1,0:T(8,128)}, u32[]{:S(2)}, u32[]{:S(2)}) collective-permute-start(f32[256,512]{1,0:T(8,128)} %slice_select_fusion), channel_id=1, source_target_pairs={{0,8},{8,0},{16,24},{24,16},{32,40},{40,32},{48,56},{56,48},{64,72... | collective-permute-start | bytes 1572872 | tf_op jit(solution)/shard_map/ppermute | solution.py:16
  125.9 7.7 %copy-start.9 = (s32[4]{0:T(128)S(1)}, s32[4]{0:T(128)}, u32[]{:S(2)}) copy-start(s32[4]{0:T(128)} %param.11) | copy-start | bytes 52
  126.8 13.2 %collective-permute-start = (f32[256,512]{1,0:T(8,128)}, f32[256,512]{1,0:T(8,128)}, u32[]{:S(2)}, u32[]{:S(2)}) collective-permute-start(f32[256,512]{1,0:T(8,128)} %slice_select_fusion.1), channel_id=1, source_target_pairs={{0,8},{8,0},{16,24},{24,16},{32,40},{40,32},{48,56},{56,48},{64,72... | collective-permute-start | bytes 1572872 | tf_op jit(solution)/shard_map/ppermute | solution.py:16
  133.6 13.3 %copy-start.3 = (bf16[2,128,8,64]{1,3,2,0:T(8,128)(2,1)}, bf16[2,128,8,64]{1,3,2,0:T(8,128)(2,1)S(1)}, u32[]{:S(2)}) copy-start(bf16[2,128,8,64]{1,3,2,0:T(8,128)(2,1)S(1)} %copy.33) | copy-start | bytes 786436
  141.9 5.0 %copy-start.5 = (bf16[2,128,8,64]{1,3,2,0:T(8,128)(2,1)S(1)}, bf16[2,128,8,64]{1,3,2,0:T(8,128)(2,1)}, u32[]{:S(2)}) copy-start(bf16[2,128,8,64]{1,3,2,0:T(8,128)(2,1)} %copy.26) | copy-start | bytes 786436
  141.9 5.0 %copy-start.6 = (bf16[2,128,8,64]{1,3,2,0:T(8,128)(2,1)S(1)}, bf16[2,128,8,64]{1,3,2,0:T(8,128)(2,1)}, u32[]{:S(2)}) copy-start(bf16[2,128,8,64]{1,3,2,0:T(8,128)(2,1)} %copy.25) | copy-start | bytes 786436
  148.0 6.5 %collective-permute-start.3 = (bf16[256,512]{0,1:T(8,128)(2,1)S(1)}, bf16[256,512]{0,1:T(8,128)(2,1)}, u32[]{:S(2)}, u32[]{:S(2)}) collective-permute-start(bf16[256,512]{0,1:T(8,128)(2,1)S(1)} %bitcast.62), channel_id=1, source_target_pairs={{0,8},{8,0},{16,24},{24,16},{32,40},{40,32},{48,56},{56,48},{64,72... | collective-permute-start | bytes 786440 | tf_op jit(solution)/shard_map/ppermute | solution.py:16
  154.0 3.6 collective-permute-start.2
  165.2 150.6 %copy-start.7 = (bf16[2,128,8,64]{1,3,2,0:T(8,128)(2,1)S(1)}, bf16[2,128,8,64]{1,3,2,0:T(8,128)(2,1)}, u32[]{:S(2)}) copy-start(bf16[2,128,8,64]{1,3,2,0:T(8,128)(2,1)} %copy.25) | copy-start | bytes 786436
  165.2 238.0 %reduce-scatter.5.cloned.1.call-start = ((), (), s32[]{:S(2)}) async-start(), calls=%async_computation.4 | async-start | bytes 294912 | tf_op jit(solution)/shard_map/reduce_scatter | solution.py:107
Sparse Core Ops, SparseCore 0:
  50.1 70.2 all-gather.1
  165.3 150.3 reduce-scatter.2
  320.1 83.0 reduce-scatter.4
where the time goes:
time: 411 us; the launch traced here: 410 us
  waiting for transfers between devices  300 us (73%)
  blocking collectives  42.8 us (10%)
  matrix products  23.1 us (6%)
  local copies, waits for them, and re-layouts  22.5 us (5%)
  between operations  13.9 us (3%)
  other arithmetic  5.97 us (1%)
    reduce_scatter x1, waiting for transfers between devices, body(): lax.psum_scatter(lax.dynamic_update_slice_in_dim(blank_rows, block, half_...  150 us
    reduce_scatter x1, waiting for transfers between devices, body(): lax.psum_scatter(layer_total, 'tensor', scatter_dimension=1, tiled=True)  79.1 us
    all_gather x1, waiting for transfers between devices, body(): lax.all_gather(full_rows, 'section', axis=0, tiled=True)  70.3 us
    all_gather x1, blocking collectives, body(): full_rows = lax.all_gather(memory, 'tensor', axis=1, tiled=True)  42.8 us
  transfers between devices with their start and end apart: 7, of which 3 were waited for; matrix products, arithmetic and copies ran while one was open for 8% of the time, Pallas kernels for 0%

commit v1 on v0

v1 whole, which is shorter than its diff:
```python
import jax
import jax.numpy as jnp
from jax import lax
from jax.experimental import pallas as pl
from jax.experimental.pallas import tpu as pltpu
from jax.sharding import Mesh, PartitionSpec as P

HDIM = 64
AXES = ("zl", "y", "core", "zh", "x")
NZ, NY, NC, NH, NX = 4, 4, 2, 2, 4
F32, BF16 = jnp.float32, jnp.bfloat16
VM = pl.BlockSpec(memory_space=pltpu.VMEM)
SM = pl.BlockSpec(memory_space=pltpu.SMEM)


def nt(a, b):
    return lax.dot_general(a, b, (((1,), (1,)), ((), ())), preferred_element_type=F32)


def nn(a, b):
    return lax.dot_general(a, b, (((1,), (0,)), ((), ())), preferred_element_type=F32)


def project_kernel(pair_ref, mem_ref, wk_ref, wv_ref, out_ref, rows_ref):
    base = pair_ref[0] * 64
    for x in range(NX):
        for i in range(2):
            start = pl.multiple_of(base + 32 * i, 32)
            part = mem_ref[:, x, pl.ds(start, 32), :].reshape(128, 512)
            rows_ref[128 * i : 128 * (i + 1), 512 * x : 512 * (x + 1)] = part
    out_ref[0] = nn(rows_ref[...], wk_ref[...])
    out_ref[1] = nn(rows_ref[...], wv_ref[...])


def project(pair, mem, wk, wv):
    return pl.pallas_call(
        project_kernel,
        out_shape=jax.ShapeDtypeStruct((2, 256, 512), F32),
        in_specs=[SM, VM, VM, VM],
        out_specs=VM,
        scratch_shapes=[pltpu.VMEM((256, 2048), BF16)],
        compiler_params=pltpu.CompilerParams(vmem_limit_bytes=20 << 20),
        cost_estimate=pl.CostEstimate(flops=2 * 2 * 256 * 2048 * 512, bytes_accessed=7 << 20, transcendentals=0),
        name="project",
    )(pair, mem, wk, wv)


def attend_kernel(pair_ref, len_ref, own_ref, got_ref, q_ref, g_ref, ctx_ref, gq_ref, gk_ref, gv_ref):
    scale = HDIM ** (-0.5)
    low = lax.broadcasted_iota(jnp.int32, (128, 128), 1) < HDIM
    token = lax.broadcasted_iota(jnp.int32, (2, 128, 128), 1)
    zero = jnp.zeros((128, 128), F32)

    def split(a):
        a = a.astype(F32)
        return jnp.concatenate([jnp.where(low, a, zero), jnp.where(low, zero, a)], axis=0).astype(BF16)

    for i in range(2):
        valid = token < len_ref[pair_ref[0] * 2 + i]
        for p in range(4):
            at = (slice(128 * i, 128 * (i + 1)), slice(128 * p, 128 * (p + 1)))
            ks = split((own_ref[0][at] + got_ref[0][at]).astype(BF16))
            vs = split((own_ref[1][at] + got_ref[1][at]).astype(BF16))
            q, g = q_ref[at], g_ref[at]
            qs, gs = split(q), split(g)
            s = nt(ks, q).reshape(2, 128, 128) * scale
            s = jnp.where(valid, s, F32(-1e30))
            e = jnp.exp(s - jnp.max(s, axis=1, keepdims=True))
            prob = e / jnp.sum(e, axis=1, keepdims=True)
            dp = nt(vs, g).reshape(2, 128, 128)
            delta = jnp.sum(prob * dp, axis=1, keepdims=True)
            ds = (prob * (dp - delta) * scale).astype(BF16)
            pb = prob.astype(BF16)
            ctx_ref[at] = nn(pb.reshape(256, 128).T, vs).astype(BF16)
            gq_ref[at] = nn(ds.reshape(256, 128).T, ks).astype(BF16)
            gk_ref[at] = nn(jnp.concatenate([ds[0], ds[1]], axis=1), qs).astype(BF16)
            gv_ref[at] = nn(jnp.concatenate([pb[0], pb[1]], axis=1), gs).astype(BF16)


def attend(pair, lengths, own, got, q, g):
    one = jax.ShapeDtypeStruct((256, 512), BF16)
    return pl.pallas_call(
        attend_kernel,
        out_shape=(one, one, one, one),
        in_specs=[SM, SM, VM, VM, VM, VM],
        out_specs=(VM, VM, VM, VM),
        compiler_params=pltpu.CompilerParams(vmem_limit_bytes=20 << 20),
        cost_estimate=pl.CostEstimate(flops=6 * 8 * 2 * 256 * 128 * 128, bytes_accessed=4 << 20, transcendentals=1 << 18),
        name="attend",
    )(pair, lengths, own, got, q, g)


def back_kernel(pair_ref, mine_ref, theirs_ref, wk_ref, wv_ref, out_ref):
    for side, ref in enumerate((mine_ref, theirs_ref)):
        pair = pair_ref[0] if side == 0 else 1 - pair_ref[0]
        for x in range(NX):
            at = slice(512 * x, 512 * (x + 1))
            r = (nt(ref[0], wk_ref[at]) + nt(ref[1], wv_ref[at])).astype(BF16)
            for i in range(2):
                start = pl.multiple_of(pair * 64 + 32 * i, 32)
                out_ref[:, x, pl.ds(start, 32), :] = r[128 * i : 128 * (i + 1)].reshape(NY, 32, 512)


def back(pair, mine, theirs, wk, wv):
    return pl.pallas_call(
        back_kernel,
        out_shape=jax.ShapeDtypeStruct((NY, NX, 128, 512), BF16),
        in_specs=[SM, VM, VM, VM, VM],
        out_specs=VM,
        compiler_params=pltpu.CompilerParams(vmem_limit_bytes=20 << 20),
        cost_estimate=pl.CostEstimate(flops=2 * 2 * 512 * 2048 * 512, bytes_accessed=7 << 20, transcendentals=0),
        name="back",
    )(pair, mine, theirs, wk, wv)


def swap_route(flip):
    return [(c * NH + h, h * NH + (c ^ flip)) for c in range(NC) for h in range(NH)]


def gather(memory):
    high = lax.axis_index("zh")
    near = lax.ppermute(memory, ("core", "zh"), swap_route(0))
    far = lax.ppermute(memory, ("core", "zh"), swap_route(1))
    first = high == 0
    both = jnp.concatenate([jnp.where(first, near, far), jnp.where(first, far, near)], axis=0)
    column = lax.all_to_all(jnp.broadcast_to(both, (NZ, 32, 512)), "zl", 0, 0)
    column = column.reshape(128, 512)
    return lax.all_to_all(jnp.broadcast_to(column, (NY * NX, 128, 512)), ("y", "x"), 0, 0)


def scatter(parts):
    high = lax.axis_index("zh")
    got = lax.all_to_all(parts, ("y", "x"), 0, 0)
    plane = jnp.sum(got.astype(F32), axis=0).astype(BF16).reshape(NZ, 32, 512)
    line = jnp.sum(lax.all_to_all(plane, "zl", 0, 0).astype(F32), axis=0)
    first = high == 0
    near = lax.ppermute(jnp.where(first, line[:16], line[16:]), ("core", "zh"), send_route(0))
    far = lax.ppermute(jnp.where(first, line[16:], line[:16]), ("core", "zh"), send_route(1))
    return near + far


def send_route(flip):
    return [(c * NH + h, (h ^ flip) * NH + c) for c in range(NC) for h in range(NH)]


def body(queries, memory, key_weight, value_weight, grad_context, memory_lengths):
    pair = lax.axis_index("core").astype(jnp.int32).reshape(1)
    mem = gather(memory).reshape(NY, NX, 128, 512)
    other = project(1 - pair, mem, key_weight, value_weight)
    got = lax.ppermute(other, "core", [(0, 1), (1, 0)])
    own = project(pair, mem, key_weight, value_weight)
    ctx, gq, gk, gv = attend(pair, memory_lengths, own, got, queries, grad_context)
    mine = jnp.stack([gk, gv])
    theirs = lax.ppermute(mine, "core", [(0, 1), (1, 0)])
    parts = back(pair, mine, theirs, key_weight, value_weight)
    return ctx, gq, scatter(parts.reshape(NY * NX, 128, 512))


def solution(mesh):
    fine = Mesh(mesh.devices.reshape(NZ, NY, NC, NH, NX), AXES)
    spec = P(("zl", "y", "core"), ("zh", "x"))
    return jax.shard_map(
        body,
        mesh=fine,
        in_specs=(spec, spec, spec, spec, spec, P()),
        out_specs=(spec, spec, spec),
        check_vma=False,
    )
```

time: 411 us -> 130 us (0.32)
  waiting for transfers between devices: 300 us -> 39.5 us
  starting transfers between devices: 1.49 us -> 27.6 us
  matrix products: 23.1 us -> 0 us
  local copies, waits for them, and re-layouts: 22.5 us -> 4.96 us
  between operations: 13.9 us -> 0.79 us
  Pallas kernels: 0 us -> 8.95 us
  other arithmetic: 5.97 us -> 1 us
    reduce_scatter x2 -> x0, waiting for transfers between devices: 230 us -> none  [the longest x1 150 us: body(): lax.psum_scatter(lax.dynamic_update_slice_in_dim(blank_rows, block, half_...]
    all_gather x1 -> x0, waiting for transfers between devices: 70.3 us -> none  [body(): lax.all_gather(full_rows, 'section', axis=0, tiled=True)]
    all_to_all x0 -> x3, blocking collectives: none -> 46.7 us  [the longest x1 31.1 us: scatter(): got = lax.all_to_all(parts, ('y', 'x'), 0, 0)]
    all_gather x1 -> x0, blocking collectives: 42.8 us -> none  [body(): full_rows = lax.all_gather(memory, 'tensor', axis=1, tiled=True)]
    all_to_all x0 -> x1, waiting for transfers between devices: none -> 32.8 us  [gather(): lax.all_to_all(jnp.broadcast_to(column, (NY * NX, 128, 512)), ('y', 'x'),...]
    dot_general x9 -> x0, matrix products: 20.5 us -> none  [the longest x2 6.37 us: times_transposed(): lax.dot_general(left, weight_rows, (((1,), (1,)), ((), ())), preferred_el...]
    ppermute x4 -> x6, starting transfers between devices: 1.37 us -> 20.8 us  [the longest x1 10.1 us: scatter(): lax.ppermute(jnp.where(first, line[:16], line[16:]), ('core', 'zh'), send...]
    reshape x8 -> x0, local copies, waits for them, and re-layouts: 13 us -> none  [the longest x2 4.1 us: body(): key_h = keys.reshape(half_react, enc_len, local_heads, HDIM)]
  transfers between devices with their start and end apart: 7 -> 7, of which waited for: 3 -> 5; matrix products, arithmetic and copies ran while one was open for 8% -> 0% of each run, Pallas kernels for 0% -> 1%
where the time goes in v1:
time: 130 us; the launch traced here: 129 us
  blocking collectives  46.7 us (36%)
  waiting for transfers between devices  39.5 us (30%)
  starting transfers between devices  27.6 us (21%)
  Pallas kernels  8.95 us (7%)
  local copies, waits for them, and re-layouts  4.96 us (4%)
    all_to_all x1, waiting for transfers between devices, gather(): lax.all_to_all(jnp.broadcast_to(column, (NY * NX, 128, 512)), ('y', 'x'),...  32.8 us
    all_to_all x1, blocking collectives, scatter(): got = lax.all_to_all(parts, ('y', 'x'), 0, 0)  31.1 us
    ppermute x1, starting transfers between devices, scatter(): lax.ppermute(jnp.where(first, line[:16], line[16:]), ('core', 'zh'), send...  10.1 us
    all_to_all x1, blocking collectives, gather(): column = lax.all_to_all(jnp.broadcast_to(both, (NZ, 32, 512)), 'zl', 0, 0)  8.45 us
    all_to_all x1, blocking collectives, scatter(): line = jnp.sum(lax.all_to_all(plane, 'zl', 0, 0).astype(F32), axis=0)  7.17 us
    ppermute x1, starting transfers between devices, gather(): near = lax.ppermute(memory, ('core', 'zh'), swap_route(0))  6.98 us
    all_to_all x1, starting transfers between devices, gather(): lax.all_to_all(jnp.broadcast_to(column, (NY * NX, 128, 512)), ('y', 'x'),...  6.75 us
    pallas_call x1, Pallas kernels, attend(): pl.pallas_call(attend_kernel, out_shape=(one, one, one, one), in_specs=[S...  4.11 us
  transfers between devices with their start and end apart: 7, of which 5 were waited for; matrix products, arithmetic and copies ran while one was open for 0% of the time, Pallas kernels for 1%

profile of v1, /device:TPU:1, one launch (start us, length us, event | category | flops | bytes accessed | tf_op | source)
XLA Modules:
  0.0 129.5 jit_solution(3095460988347594169)
XLA Ops:
  0.6 3.3 %collective-permute-start.1 = (bf16[16,512]{1,0:T(8,128)(2,1)}, bf16[16,512]{1,0:T(8,128)(2,1)S(1)}, u32[]{:S(2)}, u32[]{:S(2)}) collective-permute-start(bf16[16,512]{1,0:T(8,128)(2,1)} %param.7), channel_id=1, source_target_pairs={{0,4},{4,12},{8,0},{12,8},{1,5},{5,13},{9,1},{13,9},{2,6},{6,14},{... | collective-permute-start | bytes 49160 | tf_op jit(solution)/shard_map/ppermute | solution.py:123
  4.0 7.0 %collective-permute-start = (bf16[16,512]{1,0:T(8,128)(2,1)}, bf16[16,512]{1,0:T(8,128)(2,1)S(1)}, u32[]{:S(2)}, u32[]{:S(2)}) collective-permute-start(bf16[16,512]{1,0:T(8,128)(2,1)} %param.7), channel_id=1, source_target_pairs={{0,0},{4,8},{8,4},{12,12},{1,1},{5,9},{9,5},{13,13},{2,2},{6,10},{... | collective-permute-start | bytes 49160 | tf_op jit(solution)/shard_map/ppermute | solution.py:122
  11.0 0.0 collective-permute-done.1
  11.0 2.2 %collective-permute-done = bf16[16,512]{1,0:T(8,128)(2,1)S(1)} collective-permute-done((bf16[16,512]{1,0:T(8,128)(2,1)}, bf16[16,512]{1,0:T(8,128)(2,1)S(1)}, u32[]{:S(2)}, u32[]{:S(2)}) %collective-permute-start) | collective-permute-done | bytes 16416 | tf_op jit(solution)/shard_map/ppermute | solution.py:122
  13.2 8.4 %all_to_all.20 = bf16[4,32,512]{2,1,0:T(8,128)(2,1)S(1)} all-to-all(bf16[4,32,512]{2,1,0:T(8,128)(2,1)S(1)} %broadcast_in_dim.6), channel_id=1, replica_groups=mesh['zl'=4,'y'=4,'core'=2,'zh'=2,'x'=4] {'zl'}, dimensions={0} | all-to-all | bytes 262144 | tf_op jit(solution)/shard_map/all_to_all | solution.py:126
  21.6 1.5 %broadcast_in_dim.7 = bf16[16,128,512]{2,1,0:T(8,128)(2,1)} broadcast(bf16[128,512]{1,0:T(8,128)(2,1)S(1)} %bitcast.13), dimensions={1,2} | broadcast | bytes 2228224 | tf_op jit(solution)/shard_map/broadcast_in_dim | solution.py:128
  23.1 6.8 %all-to-all-start.1 = ((bf16[16,128,512]{2,1,0:T(8,128)(2,1)}), bf16[16,128,512]{2,1,0:T(8,128)(2,1)S(1)}, u32[]{:S(2)}, u32[]{:S(2)}) async-start(bf16[16,128,512]{2,1,0:T(8,128)(2,1)} %broadcast_in_dim.7), calls=%async_computation.1 | async-start | bytes 4194304 | tf_op jit(solution)/shard_map/all_to_all | solution.py:128
  29.9 32.8 %all-to-all-done.1 = bf16[16,128,512]{2,1,0:T(8,128)(2,1)S(1)} async-done(((bf16[16,128,512]{2,1,0:T(8,128)(2,1)}), bf16[16,128,512]{2,1,0:T(8,128)(2,1)S(1)}, u32[]{:S(2)}, u32[]{:S(2)}) %all-to-all-start.1) | async-done | bytes 2097184 | tf_op jit(solution)/shard_map/all_to_all | solution.py:128
  62.7 1.6 %copy-done = bf16[2048,512]{1,0:T(8,128)(2,1)S(1)} copy-done((bf16[2048,512]{1,0:T(8,128)(2,1)S(1)}, bf16[2048,512]{1,0:T(8,128)(2,1)}, u32[]{:S(2)}) %copy-start) | copy-done | bytes 2097176
  64.3 1.6 %copy-done.2 = bf16[2048,512]{1,0:T(8,128)(2,1)S(1)} copy-done((bf16[2048,512]{1,0:T(8,128)(2,1)S(1)}, bf16[2048,512]{1,0:T(8,128)(2,1)}, u32[]{:S(2)}) %copy-start.2) | copy-done | bytes 2097176
  65.9 1.2 project.3
  67.1 0.0 copy-start.4
  67.1 0.0 copy-start.5
  67.1 0.0 copy-start.6
  67.2 0.1 collective-permute-start.2
  67.3 0.2 copy-done.1
  67.5 1.2 project.2.own_ref
  68.7 0.0 copy-start.3
  68.7 1.2 collective-permute-done.2.got_ref
  69.9 4.1 %attend.1 = (bf16[256,512]{1,0:T(8,128)(2,1)}, bf16[256,512]{1,0:T(8,128)(2,1)}, bf16[256,512]{1,0:T(8,128)(2,1)S(1)}, bf16[256,512]{1,0:T(8,128)(2,1)S(1)}) custom-call(s32[1]{0:T(128)} %bitcast.pair_ref, s32[4]{0:T(128)S(1)} %copy-done.6, f32[2,256,512]{2,1,0:T(8,128)S(1)} %project.2.own_ref, f32[2,256,512]{2,1,0:T(8,128)S(1)} %collective-permute-done.2.got_ref, ...), custom_call_target="tpu_custom_call" | custom-call | flops 402653184 | bytes 4194304 | tf_op jit(solution)/shard_map/attend/pallas_call | solution.py:82
  74.0 0.1 pad_maximum_fusion.mine_ref
  74.1 0.2 collective-permute-start.3
  74.3 1.8 %collective-permute-done.3.theirs_ref = bf16[2,256,512]{2,1,0:T(8,128)(2,1)S(1)} collective-permute-done((bf16[2,256,512]{2,1,0:T(8,128)(2,1)S(1)}, bf16[2,256,512]{2,1,0:T(8,128)(2,1)S(1)}, u32[]{:S(2)}, u32[]{:S(2)}) %collective-permute-start.3) | collective-permute-done | bytes 524320 | tf_op jit(solution)/shard_map/ppermute | solution.py:154
  76.1 2.4 %back.1 = bf16[4,4,128,512]{3,2,1,0:T(8,128)(2,1)S(1)} custom-call(s32[1]{0:T(128)} %bitcast.pair_ref, bf16[2,256,512]{2,1,0:T(8,128)(2,1)S(1)} %pad_maximum_fusion.mine_ref, bf16[2,256,512]{2,1,0:T(8,128)(2,1)S(1)} %collective-permute-done.3.theirs_ref, bf16[2048,512]{1,0:T(8,128)(2,1)S(1)} %copy-done.1, bf16[2048,512]{1,0:T(8,128)(2,1)S(1)} %copy-done.3), custom_call_target="tpu_custom_call" | custom-call | flops 2147483648 | bytes 7340032 | tf_op jit(solution)/shard_map/back/pallas_call | solution.py:105
  78.5 31.1 %all_to_all.21 = bf16[16,128,512]{2,1,0:T(8,128)(2,1)S(1)} all-to-all(bf16[16,128,512]{2,1,0:T(8,128)(2,1)S(1)} %bitcast.9), channel_id=1, replica_groups=mesh['zl'=4,'y'=4,'core'=2,'zh'=2,'x'=4] {'y','x'}, dimensions={0} | all-to-all | bytes 4194304 | tf_op jit(solution)/shard_map/all_to_all | solution.py:133
  109.6 0.3 reduce_sum.21
  109.8 7.2 %all_to_all.22 = bf16[4,32,512]{2,1,0:T(8,128)(2,1)S(1)} all-to-all(bf16[4,32,512]{2,1,0:T(8,128)(2,1)S(1)} %bitcast.12), channel_id=1, replica_groups=mesh['zl'=4,'y'=4,'core'=2,'zh'=2,'x'=4] {'zl'}, dimensions={0} | all-to-all | bytes 262144 | tf_op jit(solution)/shard_map/all_to_all | solution.py:135
  117.1 0.1 collective-permute-start.5
  117.2 10.1 %collective-permute-start.4 = (f32[16,512]{1,0:T(8,128)S(1)}, f32[16,512]{1,0:T(8,128)S(1)}, u32[]{:S(2)}, u32[]{:S(2)}) collective-permute-start(f32[16,512]{1,0:T(8,128)S(1)} %get-tuple-element.12), channel_id=1, source_target_pairs={{0,0},{4,8},{8,4},{12,12},{1,1},{5,9},{9,5},{13,13},{2,2},{6,10},{... | collective-permute-start | bytes 98312 | tf_op jit(solution)/shard_map/ppermute | solution.py:137
  127.3 0.0 collective-permute-done.5
  127.3 1.6 %collective-permute-done.4 = f32[16,512]{1,0:T(8,128)S(1)} collective-permute-done((f32[16,512]{1,0:T(8,128)S(1)}, f32[16,512]{1,0:T(8,128)S(1)}, u32[]{:S(2)}, u32[]{:S(2)}) %collective-permute-start.4) | collective-permute-done | bytes 32800 | tf_op jit(solution)/shard_map/ppermute | solution.py:137
  128.9 0.6 add.3
  (12 shorter events, 0.1 us)
Async XLA Ops:
  0.6 10.3 %collective-permute-start.1 = (bf16[16,512]{1,0:T(8,128)(2,1)}, bf16[16,512]{1,0:T(8,128)(2,1)S(1)}, u32[]{:S(2)}, u32[]{:S(2)}) collective-permute-start(bf16[16,512]{1,0:T(8,128)(2,1)} %param.7), channel_id=1, source_target_pairs={{0,4},{4,12},{8,0},{12,8},{1,5},{5,13},{9,1},{13,9},{2,6},{6,14},{... | collective-permute-start | bytes 49160 | tf_op jit(solution)/shard_map/ppermute | solution.py:123
  4.0 9.2 %collective-permute-start = (bf16[16,512]{1,0:T(8,128)(2,1)}, bf16[16,512]{1,0:T(8,128)(2,1)S(1)}, u32[]{:S(2)}, u32[]{:S(2)}) collective-permute-start(bf16[16,512]{1,0:T(8,128)(2,1)} %param.7), channel_id=1, source_target_pairs={{0,0},{4,8},{8,4},{12,12},{1,1},{5,9},{9,5},{13,13},{2,2},{6,10},{... | collective-permute-start | bytes 49160 | tf_op jit(solution)/shard_map/ppermute | solution.py:122
  23.1 39.5 %all-to-all-start.1 = ((bf16[16,128,512]{2,1,0:T(8,128)(2,1)}), bf16[16,128,512]{2,1,0:T(8,128)(2,1)S(1)}, u32[]{:S(2)}, u32[]{:S(2)}) async-start(bf16[16,128,512]{2,1,0:T(8,128)(2,1)} %broadcast_in_dim.7), calls=%async_computation.1 | async-start | bytes 4194304 | tf_op jit(solution)/shard_map/all_to_all | solution.py:128
  62.7 1.6 %copy-start = (bf16[2048,512]{1,0:T(8,128)(2,1)S(1)}, bf16[2048,512]{1,0:T(8,128)(2,1)}, u32[]{:S(2)}) copy-start(bf16[2048,512]{1,0:T(8,128)(2,1)} %wk_ref.5) | copy-start | bytes 6291460
  64.3 1.6 %copy-start.2 = (bf16[2048,512]{1,0:T(8,128)(2,1)S(1)}, bf16[2048,512]{1,0:T(8,128)(2,1)}, u32[]{:S(2)}) copy-start(bf16[2048,512]{1,0:T(8,128)(2,1)} %wv_ref.5) | copy-start | bytes 6291460
  65.9 1.6 %copy-start.1 = (bf16[2048,512]{1,0:T(8,128)(2,1)S(1)}, bf16[2048,512]{1,0:T(8,128)(2,1)}, u32[]{:S(2)}) copy-start(bf16[2048,512]{1,0:T(8,128)(2,1)} %wk_ref.5) | copy-start | bytes 6291460
  67.1 2.8 %copy-start.4 = (bf16[256,512]{1,0:T(8,128)(2,1)S(1)}, bf16[256,512]{1,0:T(8,128)(2,1)}, u32[]{:S(2)}) copy-start(bf16[256,512]{1,0:T(8,128)(2,1)} %q_ref.1) | copy-start | bytes 786436
  67.1 2.8 %copy-start.5 = (bf16[256,512]{1,0:T(8,128)(2,1)S(1)}, bf16[256,512]{1,0:T(8,128)(2,1)}, u32[]{:S(2)}) copy-start(bf16[256,512]{1,0:T(8,128)(2,1)} %g_ref.1) | copy-start | bytes 786436
  67.1 2.8 %copy-start.6 = (s32[4]{0:T(128)S(1)}, s32[4]{0:T(128)}, u32[]{:S(2)}) copy-start(s32[4]{0:T(128)} %len_ref.1) | copy-start | bytes 52
  67.2 2.7 %collective-permute-start.2 = (f32[2,256,512]{2,1,0:T(8,128)S(1)}, f32[2,256,512]{2,1,0:T(8,128)S(1)}, u32[]{:S(2)}, u32[]{:S(2)}) collective-permute-start(f32[2,256,512]{2,1,0:T(8,128)S(1)} %project.3), channel_id=1, source_target_pairs={{0,8},{8,0},{1,9},{9,1},{2,10},{10,2},{3,11},{11,3},{4,12},{12,4},... | collective-permute-start | bytes 3145736 | tf_op jit(solution)/shard_map/ppermute | solution.py:150
  68.7 7.4 %copy-start.3 = (bf16[2048,512]{1,0:T(8,128)(2,1)S(1)}, bf16[2048,512]{1,0:T(8,128)(2,1)}, u32[]{:S(2)}) copy-start(bf16[2048,512]{1,0:T(8,128)(2,1)} %wv_ref.5) | copy-start | bytes 6291460
  74.1 2.0 %collective-permute-start.3 = (bf16[2,256,512]{2,1,0:T(8,128)(2,1)S(1)}, bf16[2,256,512]{2,1,0:T(8,128)(2,1)S(1)}, u32[]{:S(2)}, u32[]{:S(2)}) collective-permute-start(bf16[2,256,512]{2,1,0:T(8,128)(2,1)S(1)} %pad_maximum_fusion.mine_ref), channel_id=1, source_target_pairs={{0,8},{8,0},{1,9},{9,1},{2,10},{10,2},{3,11},{11,3},{4,12},{12,4},... | collective-permute-start | bytes 1572872 | tf_op jit(solution)/shard_map/ppermute | solution.py:154
  117.1 10.2 %collective-permute-start.5 = (f32[16,512]{1,0:T(8,128)S(1)}, f32[16,512]{1,0:T(8,128)S(1)}, u32[]{:S(2)}, u32[]{:S(2)}) collective-permute-start(f32[16,512]{1,0:T(8,128)S(1)} %get-tuple-element.11), channel_id=1, source_target_pairs={{0,8},{4,0},{8,12},{12,4},{1,9},{5,1},{9,13},{13,5},{2,10},{6,2},{... | collective-permute-start | bytes 98312 | tf_op jit(solution)/shard_map/ppermute | solution.py:138
  117.2 11.7 %collective-permute-start.4 = (f32[16,512]{1,0:T(8,128)S(1)}, f32[16,512]{1,0:T(8,128)S(1)}, u32[]{:S(2)}, u32[]{:S(2)}) collective-permute-start(f32[16,512]{1,0:T(8,128)S(1)} %get-tuple-element.12), channel_id=1, source_target_pairs={{0,0},{4,8},{8,4},{12,12},{1,1},{5,9},{9,5},{13,13},{2,2},{6,10},{... | collective-permute-start | bytes 98312 | tf_op jit(solution)/shard_map/ppermute | solution.py:137

commit v2 on v1

--- a/solution.py
+++ b/solution.py
@@ -1,3 +1,5 @@
+import functools
+
 import jax
 import jax.numpy as jnp
 from jax import lax
@@ -21,8 +23,8 @@
     return lax.dot_general(a, b, (((1,), (0,)), ((), ())), preferred_element_type=F32)
 
 
-def project_kernel(pair_ref, mem_ref, wk_ref, wv_ref, out_ref, rows_ref):
-    base = pair_ref[0] * 64
+def project_kernel(other, core_ref, mem_ref, wk_ref, wv_ref, out_ref, rows_ref):
+    base = (1 - core_ref[0] if other else core_ref[0]) * 64
     for x in range(NX):
         for i in range(2):
             start = pl.multiple_of(base + 32 * i, 32)
@@ -32,9 +34,9 @@
     out_ref[1] = nn(rows_ref[...], wv_ref[...])
 
 
-def project(pair, mem, wk, wv):
-    return pl.pallas_call(
-        project_kernel,
+def project(other, core, mem, wk, wv):
+    return pl.pallas_call(
+        functools.partial(project_kernel, other),
         out_shape=jax.ShapeDtypeStruct((2, 256, 512), F32),
         in_specs=[SM, VM, VM, VM],
         out_specs=VM,
@@ -42,10 +44,10 @@
         compiler_params=pltpu.CompilerParams(vmem_limit_bytes=20 << 20),
         cost_estimate=pl.CostEstimate(flops=2 * 2 * 256 * 2048 * 512, bytes_accessed=7 << 20, transcendentals=0),
         name="project",
-    )(pair, mem, wk, wv)
-
-
-def attend_kernel(pair_ref, len_ref, own_ref, got_ref, q_ref, g_ref, ctx_ref, gq_ref, gk_ref, gv_ref):
+    )(core, mem, wk, wv)
+
+
+def attend_kernel(pair_ref, len_ref, own_ref, got_ref, q_ref, g_ref, ctx_ref, gq_ref, grad_ref):
     scale = HDIM ** (-0.5)
     low = lax.broadcasted_iota(jnp.int32, (128, 128), 1) < HDIM
     token = lax.broadcasted_iota(jnp.int32, (2, 128, 128), 1)
@@ -73,17 +75,17 @@
             pb = prob.astype(BF16)
             ctx_ref[at] = nn(pb.reshape(256, 128).T, vs).astype(BF16)
             gq_ref[at] = nn(ds.reshape(256, 128).T, ks).astype(BF16)
-            gk_ref[at] = nn(jnp.concatenate([ds[0], ds[1]], axis=1), qs).astype(BF16)
-            gv_ref[at] = nn(jnp.concatenate([pb[0], pb[1]], axis=1), gs).astype(BF16)
+            grad_ref[(0, *at)] = nn(jnp.concatenate([ds[0], ds[1]], axis=1), qs).astype(BF16)
+            grad_ref[(1, *at)] = nn(jnp.concatenate([pb[0], pb[1]], axis=1), gs).astype(BF16)
 
 
 def attend(pair, lengths, own, got, q, g):
     one = jax.ShapeDtypeStruct((256, 512), BF16)
     return pl.pallas_call(
         attend_kernel,
-        out_shape=(one, one, one, one),
+        out_shape=(one, one, jax.ShapeDtypeStruct((2, 256, 512), BF16)),
         in_specs=[SM, SM, VM, VM, VM, VM],
-        out_specs=(VM, VM, VM, VM),
+        out_specs=(VM, VM, VM),
         compiler_params=pltpu.CompilerParams(vmem_limit_bytes=20 << 20),
         cost_estimate=pl.CostEstimate(flops=6 * 8 * 2 * 256 * 128 * 128, bytes_accessed=4 << 20, transcendentals=1 << 18),
         name="attend",
@@ -113,47 +115,106 @@
     )(pair, mine, theirs, wk, wv)
 
 
-def swap_route(flip):
-    return [(c * NH + h, h * NH + (c ^ flip)) for c in range(NC) for h in range(NH)]
-
-
-def gather(memory):
-    high = lax.axis_index("zh")
-    near = lax.ppermute(memory, ("core", "zh"), swap_route(0))
-    far = lax.ppermute(memory, ("core", "zh"), swap_route(1))
-    first = high == 0
-    both = jnp.concatenate([jnp.where(first, near, far), jnp.where(first, far, near)], axis=0)
-    column = lax.all_to_all(jnp.broadcast_to(both, (NZ, 32, 512)), "zl", 0, 0)
-    column = column.reshape(128, 512)
-    return lax.all_to_all(jnp.broadcast_to(column, (NY * NX, 128, 512)), ("y", "x"), 0, 0)
-
-
-def scatter(parts):
-    high = lax.axis_index("zh")
-    got = lax.all_to_all(parts, ("y", "x"), 0, 0)
-    plane = jnp.sum(got.astype(F32), axis=0).astype(BF16).reshape(NZ, 32, 512)
-    line = jnp.sum(lax.all_to_all(plane, "zl", 0, 0).astype(F32), axis=0)
-    first = high == 0
-    near = lax.ppermute(jnp.where(first, line[:16], line[16:]), ("core", "zh"), send_route(0))
-    far = lax.ppermute(jnp.where(first, line[16:], line[:16]), ("core", "zh"), send_route(1))
-    return near + far
-
-
-def send_route(flip):
-    return [(c * NH + h, (h ^ flip) * NH + c) for c in range(NC) for h in range(NH)]
+def swap(block):
+    return lax.ppermute(block, "core", [(0, 1), (1, 0)])
+
+
+def fan_kernel(core_ref, ring_ref, got_ref, out_ref):
+    core = core_ref[0]
+    for z in range(NZ):
+        for c in range(NC):
+            here = (core == c).astype(jnp.int32)
+            block = jnp.where(here == 1, ring_ref[z, core].astype(F32), got_ref[z].astype(F32)).astype(BF16)
+            for k in range(NY * NX):
+                out_ref[k, 32 * z + 16 * c : 32 * z + 16 * (c + 1), :] = block
+
+
+def fan(core, ring, got):
+    return pl.pallas_call(
+        fan_kernel,
+        out_shape=jax.ShapeDtypeStruct((NY * NX, 128, 512), BF16),
+        in_specs=[SM, VM, VM],
+        out_specs=VM,
+        compiler_params=pltpu.CompilerParams(vmem_limit_bytes=12 << 20),
+        cost_estimate=pl.CostEstimate(flops=1 << 20, bytes_accessed=3 << 20, transcendentals=0),
+        name="fan",
+    )(core, ring, got)
+
+
+def spread_kernel(core_ref, block_ref, out_ref):
+    block = block_ref[...]
+    for k in range(NZ * NH):
+        out_ref[k] = block
+
+
+def pick_kernel(core_ref, ring_ref, out_ref):
+    for z in range(NZ):
+        out_ref[z] = ring_ref[z, 1 - core_ref[0]]
+
+
+def join_kernel(core_ref, keep_ref, got_ref, out_ref):
+    for z in range(NZ):
+        out_ref[z, core_ref[0]] = keep_ref[z]
+        out_ref[z, 1 - core_ref[0]] = got_ref[z]
+
+
+def small(kernel, name, shape, *args):
+    return pl.pallas_call(
+        kernel,
+        out_shape=jax.ShapeDtypeStruct(shape, BF16),
+        in_specs=[SM] + [VM] * (len(args) - 1),
+        out_specs=VM,
+        compiler_params=pltpu.CompilerParams(vmem_limit_bytes=4 << 20),
+        cost_estimate=pl.CostEstimate(flops=0, bytes_accessed=1 << 18, transcendentals=0),
+        name=name,
+    )(*args)
+
+
+def gather(memory, core):
+    copies = small(spread_kernel, "spread", (NZ * NH, 16, 512), core, memory)
+    ring = lax.all_to_all(copies, ("zl", "zh"), 0, 0).reshape(NZ, NH, 16, 512)
+    got = swap(small(pick_kernel, "pick", (NZ, 16, 512), core, ring))
+    return lax.all_to_all(fan(core, ring, got), ("y", "x"), 0, 0)
+
+
+def fold_kernel(core_ref, parts_ref, keep_ref, send_ref):
+    core = core_ref[0]
+    for side, ref in enumerate((keep_ref, send_ref)):
+        half = core if side == 0 else 1 - core
+        for z in range(NZ):
+            start = pl.multiple_of(32 * z + 16 * half, 16)
+            ref[z] = jnp.sum(parts_ref[:, pl.ds(start, 16), :].astype(F32), axis=0).astype(BF16)
+
+
+def fold(core, parts):
+    half = jax.ShapeDtypeStruct((NZ, 16, 512), BF16)
+    return pl.pallas_call(
+        fold_kernel,
+        out_shape=(half, half),
+        in_specs=[SM, VM],
+        out_specs=(VM, VM),
+        compiler_params=pltpu.CompilerParams(vmem_limit_bytes=12 << 20),
+        cost_estimate=pl.CostEstimate(flops=1 << 20, bytes_accessed=3 << 20, transcendentals=0),
+        name="fold",
+    )(core, parts)
+
+
+def scatter(parts, core):
+    keep, send = fold(core, lax.all_to_all(parts, ("y", "x"), 0, 0))
+    ring = small(join_kernel, "join", (NZ, NH, 16, 512), core, keep, swap(send))
+    ring = lax.all_to_all(ring.reshape(NZ * NH, 16, 512), ("zl", "zh"), 0, 0)
+    return jnp.sum(ring.astype(F32), axis=0)
 
 
 def body(queries, memory, key_weight, value_weight, grad_context, memory_lengths):
-    pair = lax.axis_index("core").astype(jnp.int32).reshape(1)
-    mem = gather(memory).reshape(NY, NX, 128, 512)
-    other = project(1 - pair, mem, key_weight, value_weight)
-    got = lax.ppermute(other, "core", [(0, 1), (1, 0)])
-    own = project(pair, mem, key_weight, value_weight)
-    ctx, gq, gk, gv = attend(pair, memory_lengths, own, got, queries, grad_context)
-    mine = jnp.stack([gk, gv])
-    theirs = lax.ppermute(mine, "core", [(0, 1), (1, 0)])
-    parts = back(pair, mine, theirs, key_weight, value_weight)
-    return ctx, gq, scatter(parts.reshape(NY * NX, 128, 512))
+    core = lax.axis_index("core").astype(jnp.int32).reshape(1)
+    mem = gather(memory, core).reshape(NY, NX, 128, 512)
+    other = project(True, core, mem, key_weight, value_weight)
+    got = swap(other)
+    own = project(False, core, mem, key_weight, value_weight)
+    ctx, gq, mine = attend(core, memory_lengths, own, got, queries, grad_context)
+    parts = back(core, mine, swap(mine), key_weight, value_weight)
+    return ctx, gq, scatter(parts.reshape(NY * NX, 128, 512), core)
 
 
 def solution(mesh):

time: 130 us -> 112 us (0.86)
  blocking collectives: 46.7 us -> 89.6 us
  waiting for transfers between devices: 39.5 us -> 4.38 us
  starting transfers between devices: 27.6 us -> 6.24 us
  local copies, waits for them, and re-layouts: 4.96 us -> 0.74 us
    all_to_all x3 -> x4, blocking collectives: 46.7 us -> 89.6 us  [the longest x1 34.4 us: gather(): return lax.all_to_all(fan(core, ring, got), ('y', 'x'), 0, 0)]
    all_to_all x1 -> x0, waiting for transfers between devices: 32.8 us -> none  [gather(): lax.all_to_all(jnp.broadcast_to(column, (NY * NX, 128, 512)), ('y', 'x'),...]
    ppermute x6 -> x4, starting transfers between devices: 20.8 us -> 6.24 us  [swap(): return lax.ppermute(block, 'core', [(0, 1), (1, 0)])]
    all_to_all x1 -> x0, starting transfers between devices: 6.75 us -> none  [gather(): lax.all_to_all(jnp.broadcast_to(column, (NY * NX, 128, 512)), ('y', 'x'),...]
    unnamed x14 -> x12, local copies, waits for them, and re-layouts: 3.42 us -> 0.74 us
    ppermute x6 -> x4, waiting for transfers between devices: 6.7 us -> 4.38 us  [swap(): return lax.ppermute(block, 'core', [(0, 1), (1, 0)])]
    broadcast_in_dim x2 -> x0, local copies, waits for them, and re-layouts: 1.55 us -> none  [the longest x1 1.54 us: gather(): jnp.broadcast_to(column, (NY * NX, 128, 512))]
    pallas_call x3 -> x8, Pallas kernels: 6.59 us -> 7.08 us  [the longest x1 4.11 us: attend(): pl.pallas_call(attend_kernel, out_shape=(one, one, jax.ShapeDtypeStruct((...]
  transfers between devices with their start and end apart: 7 -> 4, of which waited for: 5 -> 4; matrix products, arithmetic and copies ran while one was open for 0% -> 0% of each run, Pallas kernels for 1% -> 1%
where the time goes in v2:
time: 112 us
  blocking collectives  89.6 us (80%)
  Pallas kernels  9.46 us (8%)
  starting transfers between devices  6.24 us (6%)
  waiting for transfers between devices  4.38 us (4%)
    all_to_all x1, blocking collectives, gather(): return lax.all_to_all(fan(core, ring, got), ('y', 'x'), 0, 0)  34.4 us
    all_to_all x1, blocking collectives, scatter(): keep, send = fold(core, lax.all_to_all(parts, ('y', 'x'), 0, 0))  30.2 us
    all_to_all x1, blocking collectives, gather(): ring = lax.all_to_all(copies, ('zl', 'zh'), 0, 0).reshape(NZ, NH, 16, 512)  15.6 us
    all_to_all x1, blocking collectives, scatter(): ring = lax.all_to_all(ring.reshape(NZ * NH, 16, 512), ('zl', 'zh'), 0, 0)  9.35 us
    ppermute x4, starting transfers between devices, swap(): return lax.ppermute(block, 'core', [(0, 1), (1, 0)])  6.24 us
    ppermute x4, waiting for transfers between devices, swap(): return lax.ppermute(block, 'core', [(0, 1), (1, 0)])  4.38 us
    pallas_call x1, Pallas kernels, attend(): pl.pallas_call(attend_kernel, out_shape=(one, one, jax.ShapeDtypeStruct((...  4.11 us
    pallas_call x2, Pallas kernels, project(): pl.pallas_call(functools.partial(project_kernel, other), out_shape=jax.Sh...  2.47 us
  transfers between devices with their start and end apart: 4, of which 4 were waited for; matrix products, arithmetic and copies ran while one was open for 0% of the time, Pallas kernels for 1%

profile of v2, /device:TPU:1, one launch (start us, length us, event | category | flops | bytes accessed | tf_op | source)
XLA Modules:
  0.0 111.8 jit_solution(7220262243683987225)
XLA Ops:
  0.6 0.0 copy-start.4
  0.6 0.7 copy-done.4
  1.4 15.6 %all_to_all.20 = bf16[8,16,512]{2,1,0:T(8,128)(2,1)S(1)} all-to-all(bf16[8,16,512]{2,1,0:T(8,128)(2,1)S(1)} %spread.1), channel_id=1, replica_groups=mesh['zl'=4,'y'=4,'core'=2,'zh'=2,'x'=4] {'zl','zh'}, dimensions={0} | all-to-all | bytes 262144 | tf_op jit(solution)/shard_map/all_to_all | solution.py:175
  17.0 2.2 %collective-permute-start = (bf16[4,16,512]{2,1,0:T(8,128)(2,1)S(1)}, bf16[4,16,512]{2,1,0:T(8,128)(2,1)S(1)}, u32[]{:S(2)}, u32[]{:S(2)}) collective-permute-start(bf16[4,16,512]{2,1,0:T(8,128)(2,1)S(1)} %pick.1), channel_id=1, source_target_pairs={{0,8},{8,0},{1,9},{9,1},{2,10},{10,2},{3,11},{11,3},{4,12},{12,4},... | collective-permute-start | bytes 196616 | tf_op jit(solution)/shard_map/ppermute | solution.py:119
  19.1 0.9 collective-permute-done.got_ref
  20.0 0.2 fan.1
  20.2 0.0 copy-start
  20.3 0.0 copy-start.1
  20.3 34.4 %all_to_all.21 = bf16[16,128,512]{2,1,0:T(8,128)(2,1)S(1)} all-to-all(bf16[16,128,512]{2,1,0:T(8,128)(2,1)S(1)} %fan.1), channel_id=1, replica_groups=mesh['zl'=4,'y'=4,'core'=2,'zh'=2,'x'=4] {'y','x'}, dimensions={0} | all-to-all | bytes 4194304 | tf_op jit(solution)/shard_map/all_to_all | solution.py:177
  54.7 0.0 copy-done
  54.7 0.0 copy-done.1
  54.7 1.2 %project.3 = f32[2,256,512]{2,1,0:T(8,128)S(1)} custom-call(s32[1]{0:T(128)} %bitcast.core_ref.pair_ref, bf16[4,4,128,512]{3,2,1,0:T(8,128)(2,1)S(1)} %bitcast.5, bf16[2048,512]{1,0:T(8,128)(2,1)S(1)} %copy-done, bf16[2048,512]{1,0:T(8,128)(2,1)S(1)} %copy-done.1), custom_call_target="tpu_custom_call" | custom-call | flops 1073741824 | bytes 7340032 | tf_op jit(solution)/shard_map/project/pallas_call | solution.py:38
  55.9 0.0 copy-start.2
  55.9 0.0 copy-start.3
  56.0 0.0 copy-start.5
  56.0 1.8 %collective-permute-start.1 = (f32[2,256,512]{2,1,0:T(8,128)S(1)}, f32[2,256,512]{2,1,0:T(8,128)S(1)}, u32[]{:S(2)}, u32[]{:S(2)}) collective-permute-start(f32[2,256,512]{2,1,0:T(8,128)S(1)} %project.3), channel_id=1, source_target_pairs={{0,8},{8,0},{1,9},{9,1},{2,10},{10,2},{3,11},{11,3},{4,12},{12,4},... | collective-permute-start | bytes 3145736 | tf_op jit(solution)/shard_map/ppermute | solution.py:119
  57.8 1.2 %project.2.own_ref = f32[2,256,512]{2,1,0:T(8,128)S(1)} custom-call(s32[1]{0:T(128)} %bitcast.core_ref.pair_ref, bf16[4,4,128,512]{3,2,1,0:T(8,128)(2,1)S(1)} %bitcast.6, bf16[2048,512]{1,0:T(8,128)(2,1)S(1)} %copy-done, bf16[2048,512]{1,0:T(8,128)(2,1)S(1)} %copy-done.1), custom_call_target="tpu_custom_call" | custom-call | flops 1073741824 | bytes 7340032 | tf_op jit(solution)/shard_map/project/pallas_call | solution.py:38
  59.0 1.0 collective-permute-done.1.got_ref
  60.1 0.0 copy-done.2
  60.1 0.0 copy-done.3
  60.1 0.0 copy-done.5
  60.1 4.1 %attend.1 = (bf16[256,512]{1,0:T(8,128)(2,1)}, bf16[256,512]{1,0:T(8,128)(2,1)}, bf16[2,256,512]{2,1,0:T(8,128)(2,1)S(1)}) custom-call(s32[1]{0:T(128)} %bitcast.core_ref.pair_ref, s32[4]{0:T(128)S(1)} %copy-done.5, f32[2,256,512]{2,1,0:T(8,128)S(1)} %project.2.own_ref, f32[2,256,512]{2,1,0:T(8,128)S(1)} %collective-permute-done.1.got_ref, ...), custom_call_target="tpu_custom_call" | custom-call | flops 402653184 | bytes 4194304 | tf_op jit(solution)/shard_map/attend/pallas_call | solution.py:84
  64.2 0.4 collective-permute-start.2
  64.6 1.5 %collective-permute-done.2.theirs_ref = bf16[2,256,512]{2,1,0:T(8,128)(2,1)S(1)} collective-permute-done((bf16[2,256,512]{2,1,0:T(8,128)(2,1)S(1)}, bf16[2,256,512]{2,1,0:T(8,128)(2,1)S(1)}, u32[]{:S(2)}, u32[]{:S(2)}) %collective-permute-start.2) | collective-permute-done | bytes 524320 | tf_op jit(solution)/shard_map/ppermute | solution.py:119
  66.1 2.4 %back.1 = bf16[4,4,128,512]{3,2,1,0:T(8,128)(2,1)S(1)} custom-call(s32[1]{0:T(128)} %bitcast.core_ref.pair_ref, bf16[2,256,512]{2,1,0:T(8,128)(2,1)S(1)} %get-tuple-element.10.mine_ref, bf16[2,256,512]{2,1,0:T(8,128)(2,1)S(1)} %collective-permute-done.2.theirs_ref, bf16[2048,512]{1,0:T(8,128)(2,1)S(1)} %copy-done, bf16[2048,512]{1,0:T(8,128)(2,1)S(1)} %copy-done.1), custom_call_target="tpu_custom_call" | custom-call | flops 2147483648 | bytes 7340032 | tf_op jit(solution)/shard_map/back/pallas_call | solution.py:107
  68.5 30.2 %all_to_all.22.parts_ref = bf16[16,128,512]{2,1,0:T(8,128)(2,1)S(1)} all-to-all(bf16[16,128,512]{2,1,0:T(8,128)(2,1)S(1)} %bitcast.7), channel_id=1, replica_groups=mesh['zl'=4,'y'=4,'core'=2,'zh'=2,'x'=4] {'y','x'}, dimensions={0} | all-to-all | bytes 4194304 | tf_op jit(solution)/shard_map/all_to_all | solution.py:203
  98.8 0.3 fold.1
  99.1 1.9 %collective-permute-start.3 = (bf16[4,16,512]{2,1,0:T(8,128)(2,1)S(1)}, bf16[4,16,512]{2,1,0:T(8,128)(2,1)S(1)}, u32[]{:S(2)}, u32[]{:S(2)}) collective-permute-start(bf16[4,16,512]{2,1,0:T(8,128)(2,1)S(1)} %get-tuple-element.12), channel_id=1, source_target_pairs={{0,8},{8,0},{1,9},{9,1},{2,10},{10,2},{3,11},{11,3},{4,12},{12,4},... | collective-permute-start | bytes 196616 | tf_op jit(solution)/shard_map/ppermute | solution.py:119
  100.9 0.9 collective-permute-done.3.got_ref
  101.8 9.3 %all_to_all.23 = bf16[8,16,512]{2,1,0:T(8,128)(2,1)S(1)} all-to-all(bf16[8,16,512]{2,1,0:T(8,128)(2,1)S(1)} %bitcast.10), channel_id=1, replica_groups=mesh['zl'=4,'y'=4,'core'=2,'zh'=2,'x'=4] {'zl','zh'}, dimensions={0} | all-to-all | bytes 262144 | tf_op jit(solution)/shard_map/all_to_all | solution.py:205
  111.2 0.6 convert_reduce_fusion
  (3 shorter events, 0.0 us)
Async XLA Ops:
  0.6 0.7 copy-start.4
  17.0 3.1 %collective-permute-start = (bf16[4,16,512]{2,1,0:T(8,128)(2,1)S(1)}, bf16[4,16,512]{2,1,0:T(8,128)(2,1)S(1)}, u32[]{:S(2)}, u32[]{:S(2)}) collective-permute-start(bf16[4,16,512]{2,1,0:T(8,128)(2,1)S(1)} %pick.1), channel_id=1, source_target_pairs={{0,8},{8,0},{1,9},{9,1},{2,10},{10,2},{3,11},{11,3},{4,12},{12,4},... | collective-permute-start | bytes 196616 | tf_op jit(solution)/shard_map/ppermute | solution.py:119
  20.2 34.4 %copy-start = (bf16[2048,512]{1,0:T(8,128)(2,1)S(1)}, bf16[2048,512]{1,0:T(8,128)(2,1)}, u32[]{:S(2)}) copy-start(bf16[2048,512]{1,0:T(8,128)(2,1)} %wk_ref.5) | copy-start | bytes 6291460
  20.3 34.4 %copy-start.1 = (bf16[2048,512]{1,0:T(8,128)(2,1)S(1)}, bf16[2048,512]{1,0:T(8,128)(2,1)}, u32[]{:S(2)}) copy-start(bf16[2048,512]{1,0:T(8,128)(2,1)} %wv_ref.5) | copy-start | bytes 6291460
  55.9 4.2 %copy-start.2 = (bf16[256,512]{1,0:T(8,128)(2,1)S(1)}, bf16[256,512]{1,0:T(8,128)(2,1)}, u32[]{:S(2)}) copy-start(bf16[256,512]{1,0:T(8,128)(2,1)} %q_ref.1) | copy-start | bytes 786436
  55.9 4.2 %copy-start.3 = (bf16[256,512]{1,0:T(8,128)(2,1)S(1)}, bf16[256,512]{1,0:T(8,128)(2,1)}, u32[]{:S(2)}) copy-start(bf16[256,512]{1,0:T(8,128)(2,1)} %g_ref.1) | copy-start | bytes 786436
  56.0 4.1 %copy-start.5 = (s32[4]{0:T(128)S(1)}, s32[4]{0:T(128)}, u32[]{:S(2)}) copy-start(s32[4]{0:T(128)} %len_ref.1) | copy-start | bytes 52
  56.0 4.1 %collective-permute-start.1 = (f32[2,256,512]{2,1,0:T(8,128)S(1)}, f32[2,256,512]{2,1,0:T(8,128)S(1)}, u32[]{:S(2)}, u32[]{:S(2)}) collective-permute-start(f32[2,256,512]{2,1,0:T(8,128)S(1)} %project.3), channel_id=1, source_target_pairs={{0,8},{8,0},{1,9},{9,1},{2,10},{10,2},{3,11},{11,3},{4,12},{12,4},... | collective-permute-start | bytes 3145736 | tf_op jit(solution)/shard_map/ppermute | solution.py:119
  64.2 1.9 %collective-permute-start.2 = (bf16[2,256,512]{2,1,0:T(8,128)(2,1)S(1)}, bf16[2,256,512]{2,1,0:T(8,128)(2,1)S(1)}, u32[]{:S(2)}, u32[]{:S(2)}) collective-permute-start(bf16[2,256,512]{2,1,0:T(8,128)(2,1)S(1)} %get-tuple-element.10.mine_ref), channel_id=1, source_target_pairs={{0,8},{8,0},{1,9},{9,1},{2,10},{10,2},{3,11},{11,3},{4,12},{12,4},... | collective-permute-start | bytes 1572872 | tf_op jit(solution)/shard_map/ppermute | solution.py:119
  99.1 2.8 %collective-permute-start.3 = (bf16[4,16,512]{2,1,0:T(8,128)(2,1)S(1)}, bf16[4,16,512]{2,1,0:T(8,128)(2,1)S(1)}, u32[]{:S(2)}, u32[]{:S(2)}) collective-permute-start(bf16[4,16,512]{2,1,0:T(8,128)(2,1)S(1)} %get-tuple-element.12), channel_id=1, source_target_pairs={{0,8},{8,0},{1,9},{9,1},{2,10},{10,2},{3,11},{11,3},{4,12},{12,4},... | collective-permute-start | bytes 196616 | tf_op jit(solution)/shard_map/ppermute | solution.py:119

commit v3 on v2

--- a/solution.py
+++ b/solution.py
@@ -23,28 +23,35 @@
     return lax.dot_general(a, b, (((1,), (0,)), ((), ())), preferred_element_type=F32)
 
 
-def project_kernel(other, core_ref, mem_ref, wk_ref, wv_ref, out_ref, rows_ref):
+def place(core, y, x, far, near):
+    return jnp.where(core == 0, y + far, y + near) % NY, jnp.where(core == 0, x + near, x + far) % NX
+
+
+def project_kernel(other, core_ref, y_ref, x_ref, b0_ref, b1_ref, b2_ref, b3_ref, wk_ref, wv_ref, out_ref, rows_ref):
     base = (1 - core_ref[0] if other else core_ref[0]) * 64
-    for x in range(NX):
-        for i in range(2):
-            start = pl.multiple_of(base + 32 * i, 32)
-            part = mem_ref[:, x, pl.ds(start, 32), :].reshape(128, 512)
-            rows_ref[128 * i : 128 * (i + 1), 512 * x : 512 * (x + 1)] = part
-    out_ref[0] = nn(rows_ref[...], wk_ref[...])
-    out_ref[1] = nn(rows_ref[...], wv_ref[...])
-
-
-def project(other, core, mem, wk, wv):
+    for far, ref in enumerate((b0_ref, b1_ref, b2_ref, b3_ref)):
+        for near in range(4):
+            y, x = place(core_ref[0], y_ref[0], x_ref[0], 4 - far, 4 - near)
+            for i in range(2):
+                start = pl.multiple_of(base + 32 * i, 32)
+                row = pl.multiple_of(128 * i + 32 * y, 32)
+                rows_ref[x, pl.ds(row, 32), :] = ref[near, pl.ds(start, 32), :]
+    rows = jnp.concatenate([rows_ref[x] for x in range(NX)], axis=1)
+    out_ref[0] = nn(rows, wk_ref[...])
+    out_ref[1] = nn(rows, wv_ref[...])
+
+
+def project(other, here, blocks, wk, wv):
     return pl.pallas_call(
         functools.partial(project_kernel, other),
         out_shape=jax.ShapeDtypeStruct((2, 256, 512), F32),
-        in_specs=[SM, VM, VM, VM],
+        in_specs=[SM] * 3 + [VM] * 6,
         out_specs=VM,
-        scratch_shapes=[pltpu.VMEM((256, 2048), BF16)],
+        scratch_shapes=[pltpu.VMEM((NX, 256, 512), BF16)],
         compiler_params=pltpu.CompilerParams(vmem_limit_bytes=20 << 20),
         cost_estimate=pl.CostEstimate(flops=2 * 2 * 256 * 2048 * 512, bytes_accessed=7 << 20, transcendentals=0),
         name="project",
-    )(core, mem, wk, wv)
+    )(*here, *blocks, wk, wv)
 
 
 def attend_kernel(pair_ref, len_ref, own_ref, got_ref, q_ref, g_ref, ctx_ref, gq_ref, grad_ref):
@@ -92,53 +99,90 @@
     )(pair, lengths, own, got, q, g)
 
 
-def back_kernel(pair_ref, mine_ref, theirs_ref, wk_ref, wv_ref, out_ref):
+def stage_kernel(wk_ref, wv_ref, after_ref, k_ref, v_ref, sems):
+    copies = [
+        pltpu.make_async_copy(wk_ref, k_ref, sems.at[0]),
+        pltpu.make_async_copy(wv_ref, v_ref, sems.at[1]),
+    ]
+    for copy in copies:
+        copy.start()
+    for copy in copies:
+        copy.wait()
+
+
+def stage(wk, wv, after):
+    leave = pl.BlockSpec(memory_space=pl.ANY)
+    return pl.pallas_call(
+        stage_kernel,
+        out_shape=(jax.ShapeDtypeStruct(wk.shape, BF16), jax.ShapeDtypeStruct(wv.shape, BF16)),
+        in_specs=[leave, leave, leave],
+        out_specs=(VM, VM),
+        scratch_shapes=[pltpu.SemaphoreType.DMA((2,))],
+        compiler_params=pltpu.CompilerParams(vmem_limit_bytes=10 << 20),
+        cost_estimate=pl.CostEstimate(flops=0, bytes_accessed=8 << 20, transcendentals=0),
+        name="stage",
+    )(wk, wv, after)
+
+
+def back_kernel(core_ref, y_ref, x_ref, mine_ref, theirs_ref, wk_ref, wv_ref, o0_ref, o1_ref, o2_ref, o3_ref, all_ref):
     for side, ref in enumerate((mine_ref, theirs_ref)):
-        pair = pair_ref[0] if side == 0 else 1 - pair_ref[0]
+        pair = core_ref[0] if side == 0 else 1 - core_ref[0]
         for x in range(NX):
             at = slice(512 * x, 512 * (x + 1))
             r = (nt(ref[0], wk_ref[at]) + nt(ref[1], wv_ref[at])).astype(BF16)
             for i in range(2):
                 start = pl.multiple_of(pair * 64 + 32 * i, 32)
-                out_ref[:, x, pl.ds(start, 32), :] = r[128 * i : 128 * (i + 1)].reshape(NY, 32, 512)
-
-
-def back(pair, mine, theirs, wk, wv):
+                all_ref[:, x, pl.ds(start, 32), :] = r[128 * i : 128 * (i + 1)].reshape(NY, 32, 512)
+    for far, ref in enumerate((o0_ref, o1_ref, o2_ref, o3_ref)):
+        for near in range(4):
+            y, x = place(core_ref[0], y_ref[0], x_ref[0], far, near)
+            ref[near] = all_ref[y, x]
+
+
+def back(here, mine, theirs, wk, wv):
+    part = jax.ShapeDtypeStruct((4, 128, 512), BF16)
     return pl.pallas_call(
         back_kernel,
-        out_shape=jax.ShapeDtypeStruct((NY, NX, 128, 512), BF16),
-        in_specs=[SM, VM, VM, VM, VM],
-        out_specs=VM,
+        out_shape=(part, part, part, part),
+        in_specs=[SM] * 3 + [VM] * 4,
+        out_specs=(VM, VM, VM, VM),
+        scratch_shapes=[pltpu.VMEM((NY, NX, 128, 512), BF16)],
         compiler_params=pltpu.CompilerParams(vmem_limit_bytes=20 << 20),
         cost_estimate=pl.CostEstimate(flops=2 * 2 * 512 * 2048 * 512, bytes_accessed=7 << 20, transcendentals=0),
         name="back",
-    )(pair, mine, theirs, wk, wv)
+    )(*here, mine, theirs, wk, wv)
 
 
 def swap(block):
     return lax.ppermute(block, "core", [(0, 1), (1, 0)])
 
 
-def fan_kernel(core_ref, ring_ref, got_ref, out_ref):
+def route(along, shift):
+    pairs = []
+    for y in range(NY):
+        for c in range(NC):
+            for x in range(NX):
+                to = (y, (x + shift) % NX) if c == along else ((y + shift) % NY, x)
+                pairs.append(((y * NC + c) * NX + x, (to[0] * NC + c) * NX + to[1]))
+    return pairs
+
+
+def shifted(along, blocks):
+    return [lax.ppermute(b, ("y", "core", "x"), route(along, k)) for k, b in zip((1, 2, 3), blocks)]
+
+
+def column_kernel(core_ref, ring_ref, got_ref, out_ref):
     core = core_ref[0]
     for z in range(NZ):
-        for c in range(NC):
-            here = (core == c).astype(jnp.int32)
-            block = jnp.where(here == 1, ring_ref[z, core].astype(F32), got_ref[z].astype(F32)).astype(BF16)
-            for k in range(NY * NX):
-                out_ref[k, 32 * z + 16 * c : 32 * z + 16 * (c + 1), :] = block
-
-
-def fan(core, ring, got):
-    return pl.pallas_call(
-        fan_kernel,
-        out_shape=jax.ShapeDtypeStruct((NY * NX, 128, 512), BF16),
-        in_specs=[SM, VM, VM],
-        out_specs=VM,
-        compiler_params=pltpu.CompilerParams(vmem_limit_bytes=12 << 20),
-        cost_estimate=pl.CostEstimate(flops=1 << 20, bytes_accessed=3 << 20, transcendentals=0),
-        name="fan",
-    )(core, ring, got)
+        own = pl.multiple_of(32 * z + 16 * core, 16)
+        out_ref[pl.ds(own, 16), :] = ring_ref[z, core]
+        other = pl.multiple_of(32 * z + 16 * (1 - core), 16)
+        out_ref[pl.ds(other, 16), :] = got_ref[z]
+
+
+def pack_kernel(core_ref, *refs):
+    for k in range(4):
+        refs[4][k] = refs[k][...]
 
 
 def spread_kernel(core_ref, block_ref, out_ref):
@@ -174,16 +218,38 @@
     copies = small(spread_kernel, "spread", (NZ * NH, 16, 512), core, memory)
     ring = lax.all_to_all(copies, ("zl", "zh"), 0, 0).reshape(NZ, NH, 16, 512)
     got = swap(small(pick_kernel, "pick", (NZ, 16, 512), core, ring))
-    return lax.all_to_all(fan(core, ring, got), ("y", "x"), 0, 0)
-
-
-def fold_kernel(core_ref, parts_ref, keep_ref, send_ref):
+    column = small(column_kernel, "column", (128, 512), core, ring, got)
+    blocks = small(pack_kernel, "pack", (4, 128, 512), core, column, *shifted(0, [column] * 3))
+    return [blocks, *shifted(1, [blocks] * 3)]
+
+
+def total_kernel(p0_ref, p1_ref, p2_ref, p3_ref, *out_refs):
+    for near, ref in enumerate(out_refs):
+        total = p0_ref[near].astype(F32) + p1_ref[near].astype(F32)
+        ref[...] = (total + p2_ref[near].astype(F32) + p3_ref[near].astype(F32)).astype(BF16)
+
+
+def total(parts):
+    one = jax.ShapeDtypeStruct((128, 512), BF16)
+    return pl.pallas_call(
+        total_kernel,
+        out_shape=(one, one, one, one),
+        in_specs=[VM] * 4,
+        out_specs=(VM,) * 4,
+        compiler_params=pltpu.CompilerParams(vmem_limit_bytes=8 << 20),
+        cost_estimate=pl.CostEstimate(flops=1 << 20, bytes_accessed=5 << 19, transcendentals=0),
+        name="total",
+    )(*parts)
+
+
+def fold_kernel(core_ref, p0_ref, p1_ref, p2_ref, p3_ref, keep_ref, send_ref):
     core = core_ref[0]
-    for side, ref in enumerate((keep_ref, send_ref)):
+    for side, out in enumerate((keep_ref, send_ref)):
         half = core if side == 0 else 1 - core
         for z in range(NZ):
-            start = pl.multiple_of(32 * z + 16 * half, 16)
-            ref[z] = jnp.sum(parts_ref[:, pl.ds(start, 16), :].astype(F32), axis=0).astype(BF16)
+            at = pl.ds(pl.multiple_of(32 * z + 16 * half, 16), 16)
+            total = p0_ref[at, :].astype(F32) + p1_ref[at, :].astype(F32)
+            out[z] = (total + p2_ref[at, :].astype(F32) + p3_ref[at, :].astype(F32)).astype(BF16)
 
 
 def fold(core, parts):
@@ -191,30 +257,33 @@
     return pl.pallas_call(
         fold_kernel,
         out_shape=(half, half),
-        in_specs=[SM, VM],
+        in_specs=[SM] + [VM] * 4,
         out_specs=(VM, VM),
-        compiler_params=pltpu.CompilerParams(vmem_limit_bytes=12 << 20),
-        cost_estimate=pl.CostEstimate(flops=1 << 20, bytes_accessed=3 << 20, transcendentals=0),
+        compiler_params=pltpu.CompilerParams(vmem_limit_bytes=4 << 20),
+        cost_estimate=pl.CostEstimate(flops=1 << 18, bytes_accessed=1 << 19, transcendentals=0),
         name="fold",
-    )(core, parts)
+    )(core, *parts)
 
 
 def scatter(parts, core):
-    keep, send = fold(core, lax.all_to_all(parts, ("y", "x"), 0, 0))
+    line = total([parts[0], *shifted(1, parts[1:])])
+    keep, send = fold(core, [line[0], *shifted(0, line[1:])])
     ring = small(join_kernel, "join", (NZ, NH, 16, 512), core, keep, swap(send))
     ring = lax.all_to_all(ring.reshape(NZ * NH, 16, 512), ("zl", "zh"), 0, 0)
     return jnp.sum(ring.astype(F32), axis=0)
 
 
 def body(queries, memory, key_weight, value_weight, grad_context, memory_lengths):
-    core = lax.axis_index("core").astype(jnp.int32).reshape(1)
-    mem = gather(memory, core).reshape(NY, NX, 128, 512)
-    other = project(True, core, mem, key_weight, value_weight)
+    here = [lax.axis_index(name).astype(jnp.int32).reshape(1) for name in ("core", "y", "x")]
+    core = here[0]
+    blocks = gather(memory, core)
+    key_weight, value_weight = stage(key_weight, value_weight, blocks[0])
+    other = project(True, here, blocks, key_weight, value_weight)
     got = swap(other)
-    own = project(False, core, mem, key_weight, value_weight)
+    own = project(False, here, blocks, key_weight, value_weight)
     ctx, gq, mine = attend(core, memory_lengths, own, got, queries, grad_context)
-    parts = back(core, mine, swap(mine), key_weight, value_weight)
-    return ctx, gq, scatter(parts.reshape(NY * NX, 128, 512), core)
+    parts = back(here, mine, swap(mine), key_weight, value_weight)
+    return ctx, gq, scatter(parts, core)
 
 
 def solution(mesh):

time: 112 us -> 101 us (0.902)
  blocking collectives: 89.6 us -> 25 us
  waiting for transfers between devices: 4.38 us -> 38.8 us
  starting transfers between devices: 6.24 us -> 21.2 us
  local copies, waits for them, and re-layouts: 0.74 us -> 3.91 us
    all_to_all x2 -> x0, blocking collectives: 64.7 us -> none  [the longest x1 34.4 us: gather(): return lax.all_to_all(fan(core, ring, got), ('y', 'x'), 0, 0)]
    ppermute x0 -> x12, waiting for transfers between devices: none -> 34.6 us  [shifted(): lax.ppermute(b, ('y', 'core', 'x'), route(along, k))]
    ppermute x0 -> x12, starting transfers between devices: none -> 12.9 us  [shifted(): lax.ppermute(b, ('y', 'core', 'x'), route(along, k))]
    unnamed x12, local copies, waits for them, and re-layouts: 0.74 us -> 3.91 us
    ppermute x4, starting transfers between devices: 6.24 us -> 8.27 us  [swap(): return lax.ppermute(block, 'core', [(0, 1), (1, 0)])]
    pallas_call x3 -> x4, Pallas kernels: 2.86 us -> 3.17 us  [the longest x1 2.52 us: back(): pl.pallas_call(back_kernel, out_shape=(part, part, part, part), in_specs=...]
  transfers between devices with their start and end apart: 4 -> 16, of which waited for: 4 -> 13; matrix products, arithmetic and copies ran while one was open for 0% -> 0% of each run, Pallas kernels for 1% -> 2%
where the time goes in v3:
time: 101 us; the launch traced here: 100 us
  waiting for transfers between devices  38.8 us (38%)
  blocking collectives  25 us (25%)
  starting transfers between devices  21.2 us (21%)
  Pallas kernels  10.1 us (10%)
  local copies, waits for them, and re-layouts  3.91 us (4%)
    ppermute x12, waiting for transfers between devices, shifted(): lax.ppermute(b, ('y', 'core', 'x'), route(along, k))  34.6 us
    all_to_all x1, blocking collectives, gather(): ring = lax.all_to_all(copies, ('zl', 'zh'), 0, 0).reshape(NZ, NH, 16, 512)  15.6 us
    ppermute x12, starting transfers between devices, shifted(): lax.ppermute(b, ('y', 'core', 'x'), route(along, k))  12.9 us
    all_to_all x1, blocking collectives, scatter(): ring = lax.all_to_all(ring.reshape(NZ * NH, 16, 512), ('zl', 'zh'), 0, 0)  9.35 us
    ppermute x4, starting transfers between devices, swap(): return lax.ppermute(block, 'core', [(0, 1), (1, 0)])  8.27 us
    ppermute x4, waiting for transfers between devices, swap(): return lax.ppermute(block, 'core', [(0, 1), (1, 0)])  4.25 us
    pallas_call x1, Pallas kernels, attend(): pl.pallas_call(attend_kernel, out_shape=(one, one, jax.ShapeDtypeStruct((...  4.13 us
    unnamed x12, local copies, waits for them, and re-layouts  3.91 us
  transfers between devices with their start and end apart: 16, of which 13 were waited for; matrix products, arithmetic and copies ran while one was open for 0% of the time, Pallas kernels for 2%

profile of v3, /device:TPU:1, one launch (start us, length us, event | category | flops | bytes accessed | tf_op | source)
XLA Modules:
  0.0 100.4 jit_solution(962650947561390992)
XLA Ops:
  0.6 0.7 copy-done.4
  1.4 15.6 %all_to_all.10 = bf16[8,16,512]{2,1,0:T(8,128)(2,1)S(1)} all-to-all(bf16[8,16,512]{2,1,0:T(8,128)(2,1)S(1)} %spread.1), channel_id=1, replica_groups=mesh['zl'=4,'y'=4,'core'=2,'zh'=2,'x'=4] {'zl','zh'}, dimensions={0} | all-to-all | bytes 262144 | tf_op jit(solution)/shard_map/all_to_all | solution.py:219
  17.0 2.2 %collective-permute-start = (bf16[4,16,512]{2,1,0:T(8,128)(2,1)S(1)}, bf16[4,16,512]{2,1,0:T(8,128)(2,1)S(1)}, u32[]{:S(2)}, u32[]{:S(2)}) collective-permute-start(bf16[4,16,512]{2,1,0:T(8,128)(2,1)S(1)} %pick.1), channel_id=1, source_target_pairs={{0,8},{8,0},{1,9},{9,1},{2,10},{10,2},{3,11},{11,3},{4,12},{12,4},... | collective-permute-start | bytes 196616 | tf_op jit(solution)/shard_map/ppermute | solution.py:157
  19.1 0.9 collective-permute-done.got_ref
  20.1 2.8 %collective-permute-start.3 = (bf16[128,512]{1,0:T(8,128)(2,1)S(1)}, bf16[128,512]{1,0:T(8,128)(2,1)S(1)}, u32[]{:S(2)}, u32[]{:S(2)}) collective-permute-start(bf16[128,512]{1,0:T(8,128)(2,1)S(1)} %column.1.refs_0_), channel_id=1, source_target_pairs={{0,3},{1,0},{2,1},{3,2},{8,56},{9,57},{10,58},{11,59},{16,19},{17,... | collective-permute-start | bytes 393224 | tf_op jit(solution)/shard_map/ppermute | solution.py:171
  23.2 0.7 collective-permute-start.1
  23.9 2.3 %collective-permute-done.3.refs_3_ = bf16[128,512]{1,0:T(8,128)(2,1)S(1)} collective-permute-done((bf16[128,512]{1,0:T(8,128)(2,1)S(1)}, bf16[128,512]{1,0:T(8,128)(2,1)S(1)}, u32[]{:S(2)}, u32[]{:S(2)}) %collective-permute-start.3) | collective-permute-done | bytes 131104 | tf_op jit(solution)/shard_map/ppermute | solution.py:171
  26.2 2.3 %collective-permute-done.2.refs_2_ = bf16[128,512]{1,0:T(8,128)(2,1)S(1)} collective-permute-done((bf16[128,512]{1,0:T(8,128)(2,1)S(1)}, bf16[128,512]{1,0:T(8,128)(2,1)S(1)}, u32[]{:S(2)}, u32[]{:S(2)}) %collective-permute-start.2) | collective-permute-done | bytes 131104 | tf_op jit(solution)/shard_map/ppermute | solution.py:171
  28.5 1.4 %collective-permute-done.1.refs_1_ = bf16[128,512]{1,0:T(8,128)(2,1)S(1)} collective-permute-done((bf16[128,512]{1,0:T(8,128)(2,1)S(1)}, bf16[128,512]{1,0:T(8,128)(2,1)S(1)}, u32[]{:S(2)}, u32[]{:S(2)}) %collective-permute-start.1) | collective-permute-done | bytes 131104 | tf_op jit(solution)/shard_map/ppermute | solution.py:171
  29.9 2.3 %collective-permute-start.6 = (bf16[4,128,512]{2,1,0:T(8,128)(2,1)S(1)}, bf16[4,128,512]{2,1,0:T(8,128)(2,1)S(1)}, u32[]{:S(2)}, u32[]{:S(2)}) collective-permute-start(bf16[4,128,512]{2,1,0:T(8,128)(2,1)S(1)} %pack.1.after_ref.b0_ref), channel_id=1, source_target_pairs={{0,48},{1,49},{2,50},{3,51},{8,11},{9,8},{10,9},{11,10},{16,0},{17... | collective-permute-start | bytes 1572872 | tf_op jit(solution)/shard_map/ppermute | solution.py:171
  33.3 1.6 %copy-done = bf16[2048,512]{1,0:T(8,128)(2,1)S(1)} copy-done((bf16[2048,512]{1,0:T(8,128)(2,1)S(1)}, bf16[2048,512]{1,0:T(8,128)(2,1)}, u32[]{:S(2)}) %copy-start) | copy-done | bytes 2097176
  34.9 1.6 %copy-done.1 = bf16[2048,512]{1,0:T(8,128)(2,1)S(1)} copy-done((bf16[2048,512]{1,0:T(8,128)(2,1)S(1)}, bf16[2048,512]{1,0:T(8,128)(2,1)}, u32[]{:S(2)}) %copy-start.1) | copy-done | bytes 2097176
  36.8 7.1 %collective-permute-done.6.b3_ref = bf16[4,128,512]{2,1,0:T(8,128)(2,1)S(1)} collective-permute-done((bf16[4,128,512]{2,1,0:T(8,128)(2,1)S(1)}, bf16[4,128,512]{2,1,0:T(8,128)(2,1)S(1)}, u32[]{:S(2)}, u32[]{:S(2)}) %collective-permute-start.6) | collective-permute-done | bytes 524320 | tf_op jit(solution)/shard_map/ppermute | solution.py:171
  43.9 3.7 %collective-permute-done.4.b1_ref = bf16[4,128,512]{2,1,0:T(8,128)(2,1)S(1)} collective-permute-done((bf16[4,128,512]{2,1,0:T(8,128)(2,1)S(1)}, bf16[4,128,512]{2,1,0:T(8,128)(2,1)S(1)}, u32[]{:S(2)}, u32[]{:S(2)}) %collective-permute-start.4) | collective-permute-done | bytes 524320 | tf_op jit(solution)/shard_map/ppermute | solution.py:171
  47.6 1.4 %project.3 = f32[2,256,512]{2,1,0:T(8,128)S(1)} custom-call(s32[1]{0:T(128)} %bitcast.core_ref.pair_ref, s32[1]{0:T(128)} %bitcast.1.y_ref, s32[1]{0:T(128)} %bitcast.2.x_ref, bf16[4,128,512]{2,1,0:T(8,128)(2,1)S(1)} %pack.1.after_ref.b0_ref, bf16[4,128,512]{2,1,0:T(8,128)(2,1)S(1)} %collective-permute-done.4.b1_ref, ...), custom_call_target="tpu_custom_call" | custom-call | flops 1073741824 | bytes 7340032 | tf_op jit(solution)/shard_map/project/pallas_call | solution.py:45
  49.1 3.0 %collective-permute-start.7 = (f32[2,256,512]{2,1,0:T(8,128)S(1)}, f32[2,256,512]{2,1,0:T(8,128)S(1)}, u32[]{:S(2)}, u32[]{:S(2)}) collective-permute-start(f32[2,256,512]{2,1,0:T(8,128)S(1)} %project.3), channel_id=1, source_target_pairs={{0,8},{8,0},{1,9},{9,1},{2,10},{10,2},{3,11},{11,3},{4,12},{12,4},... | collective-permute-start | bytes 3145736 | tf_op jit(solution)/shard_map/ppermute | solution.py:157
  52.1 1.4 %project.2.own_ref = f32[2,256,512]{2,1,0:T(8,128)S(1)} custom-call(s32[1]{0:T(128)} %bitcast.core_ref.pair_ref, s32[1]{0:T(128)} %bitcast.1.y_ref, s32[1]{0:T(128)} %bitcast.2.x_ref, bf16[4,128,512]{2,1,0:T(8,128)(2,1)S(1)} %pack.1.after_ref.b0_ref, bf16[4,128,512]{2,1,0:T(8,128)(2,1)S(1)} %collective-permute-done.4.b1_ref, ...), custom_call_target="tpu_custom_call" | custom-call | flops 1073741824 | bytes 7340032 | tf_op jit(solution)/shard_map/project/pallas_call | solution.py:45
  53.4 0.9 collective-permute-done.7.got_ref
  54.4 4.1 %attend.1 = (bf16[256,512]{1,0:T(8,128)(2,1)}, bf16[256,512]{1,0:T(8,128)(2,1)}, bf16[2,256,512]{2,1,0:T(8,128)(2,1)S(1)}) custom-call(s32[1]{0:T(128)} %bitcast.core_ref.pair_ref, s32[4]{0:T(128)S(1)} %copy-done.5, f32[2,256,512]{2,1,0:T(8,128)S(1)} %project.2.own_ref, f32[2,256,512]{2,1,0:T(8,128)S(1)} %collective-permute-done.7.got_ref, ...), custom_call_target="tpu_custom_call" | custom-call | flops 402653184 | bytes 4194304 | tf_op jit(solution)/shard_map/attend/pallas_call | solution.py:91
  58.9 1.5 %collective-permute-done.8.theirs_ref = bf16[2,256,512]{2,1,0:T(8,128)(2,1)S(1)} collective-permute-done((bf16[2,256,512]{2,1,0:T(8,128)(2,1)S(1)}, bf16[2,256,512]{2,1,0:T(8,128)(2,1)S(1)}, u32[]{:S(2)}, u32[]{:S(2)}) %collective-permute-start.8) | collective-permute-done | bytes 524320 | tf_op jit(solution)/shard_map/ppermute | solution.py:157
  60.4 2.5 %back.1 = (bf16[4,128,512]{2,1,0:T(8,128)(2,1)S(1)}, bf16[4,128,512]{2,1,0:T(8,128)(2,1)S(1)}, bf16[4,128,512]{2,1,0:T(8,128)(2,1)S(1)}, bf16[4,128,512]{2,1,0:T(8,128)(2,1)S(1)}) custom-call(s32[1]{0:T(128)} %bitcast.core_ref.pair_ref, s32[1]{0:T(128)} %bitcast.1.y_ref, s32[1]{0:T(128)} %bitcast.2.x_ref, ...), custom_call_target="tpu_custom_call" | custom-call | flops 2147483648 | bytes 7340032 | tf_op jit(solution)/shard_map/back/pallas_call | solution.py:144
  63.2 1.4 %collective-permute-start.10 = (bf16[4,128,512]{2,1,0:T(8,128)(2,1)S(1)}, bf16[4,128,512]{2,1,0:T(8,128)(2,1)S(1)}, u32[]{:S(2)}, u32[]{:S(2)}) collective-permute-start(bf16[4,128,512]{2,1,0:T(8,128)(2,1)S(1)} %get-tuple-element.25), channel_id=1, source_target_pairs={{0,32},{1,33},{2,34},{3,35},{8,10},{9,11},{10,8},{11,9},{16,48},{1... | collective-permute-start | bytes 1572872 | tf_op jit(solution)/shard_map/ppermute | solution.py:171
  64.6 1.2 %collective-permute-start.11 = (bf16[4,128,512]{2,1,0:T(8,128)(2,1)S(1)}, bf16[4,128,512]{2,1,0:T(8,128)(2,1)S(1)}, u32[]{:S(2)}, u32[]{:S(2)}) collective-permute-start(bf16[4,128,512]{2,1,0:T(8,128)(2,1)S(1)} %get-tuple-element.26), channel_id=1, source_target_pairs={{0,48},{1,49},{2,50},{3,51},{8,11},{9,8},{10,9},{11,10},{16,0},{17... | collective-permute-start | bytes 1572872 | tf_op jit(solution)/shard_map/ppermute | solution.py:171
  65.9 12.5 %collective-permute-done.9.p1_ref = bf16[4,128,512]{2,1,0:T(8,128)(2,1)S(1)} collective-permute-done((bf16[4,128,512]{2,1,0:T(8,128)(2,1)S(1)}, bf16[4,128,512]{2,1,0:T(8,128)(2,1)S(1)}, u32[]{:S(2)}, u32[]{:S(2)}) %collective-permute-start.9) | collective-permute-done | bytes 524320 | tf_op jit(solution)/shard_map/ppermute | solution.py:171
  79.3 1.5 %collective-permute-start.13 = (bf16[128,512]{1,0:T(8,128)(2,1)S(1)}, bf16[128,512]{1,0:T(8,128)(2,1)S(1)}, u32[]{:S(2)}, u32[]{:S(2)}) collective-permute-start(bf16[128,512]{1,0:T(8,128)(2,1)S(1)} %get-tuple-element.29), channel_id=1, source_target_pairs={{0,2},{1,3},{2,0},{3,1},{8,40},{9,41},{10,42},{11,43},{16,18},{17,... | collective-permute-start | bytes 393224 | tf_op jit(solution)/shard_map/ppermute | solution.py:171
  80.8 1.2 %collective-permute-start.14 = (bf16[128,512]{1,0:T(8,128)(2,1)S(1)}, bf16[128,512]{1,0:T(8,128)(2,1)S(1)}, u32[]{:S(2)}, u32[]{:S(2)}) collective-permute-start(bf16[128,512]{1,0:T(8,128)(2,1)S(1)} %get-tuple-element.30), channel_id=1, source_target_pairs={{0,3},{1,0},{2,1},{3,2},{8,56},{9,57},{10,58},{11,59},{16,19},{17,... | collective-permute-start | bytes 393224 | tf_op jit(solution)/shard_map/ppermute | solution.py:171
  82.0 4.0 %collective-permute-done.12.p1_ref = bf16[128,512]{1,0:T(8,128)(2,1)S(1)} collective-permute-done((bf16[128,512]{1,0:T(8,128)(2,1)S(1)}, bf16[128,512]{1,0:T(8,128)(2,1)S(1)}, u32[]{:S(2)}, u32[]{:S(2)}) %collective-permute-start.12) | collective-permute-done | bytes 131104 | tf_op jit(solution)/shard_map/ppermute | solution.py:171
  86.0 0.6 collective-permute-done.14.p3_ref
  86.7 2.7 %collective-permute-start.15 = (bf16[4,16,512]{2,1,0:T(8,128)(2,1)S(1)}, bf16[4,16,512]{2,1,0:T(8,128)(2,1)S(1)}, u32[]{:S(2)}, u32[]{:S(2)}) collective-permute-start(bf16[4,16,512]{2,1,0:T(8,128)(2,1)S(1)} %get-tuple-element.32), channel_id=1, source_target_pairs={{0,8},{8,0},{1,9},{9,1},{2,10},{10,2},{3,11},{11,3},{4,12},{12,4},... | collective-permute-start | bytes 196616 | tf_op jit(solution)/shard_map/ppermute | solution.py:157
  89.5 0.9 collective-permute-done.15.got_ref
  90.4 9.3 %all_to_all.11 = bf16[8,16,512]{2,1,0:T(8,128)(2,1)S(1)} all-to-all(bf16[8,16,512]{2,1,0:T(8,128)(2,1)S(1)} %bitcast.7), channel_id=1, replica_groups=mesh['zl'=4,'y'=4,'core'=2,'zh'=2,'x'=4] {'zl','zh'}, dimensions={0} | all-to-all | bytes 262144 | tf_op jit(solution)/shard_map/all_to_all | solution.py:272
  99.7 0.6 convert_reduce_fusion
  (27 shorter events, 3.6 us)
Async XLA Ops:
  0.6 0.7 copy-start.4
  17.0 3.1 %collective-permute-start = (bf16[4,16,512]{2,1,0:T(8,128)(2,1)S(1)}, bf16[4,16,512]{2,1,0:T(8,128)(2,1)S(1)}, u32[]{:S(2)}, u32[]{:S(2)}) collective-permute-start(bf16[4,16,512]{2,1,0:T(8,128)(2,1)S(1)} %pick.1), channel_id=1, source_target_pairs={{0,8},{8,0},{1,9},{9,1},{2,10},{10,2},{3,11},{11,3},{4,12},{12,4},... | collective-permute-start | bytes 196616 | tf_op jit(solution)/shard_map/ppermute | solution.py:157
  20.1 6.1 %collective-permute-start.3 = (bf16[128,512]{1,0:T(8,128)(2,1)S(1)}, bf16[128,512]{1,0:T(8,128)(2,1)S(1)}, u32[]{:S(2)}, u32[]{:S(2)}) collective-permute-start(bf16[128,512]{1,0:T(8,128)(2,1)S(1)} %column.1.refs_0_), channel_id=1, source_target_pairs={{0,3},{1,0},{2,1},{3,2},{8,56},{9,57},{10,58},{11,59},{16,19},{17,... | collective-permute-start | bytes 393224 | tf_op jit(solution)/shard_map/ppermute | solution.py:171
  22.9 5.6 %collective-permute-start.2 = (bf16[128,512]{1,0:T(8,128)(2,1)S(1)}, bf16[128,512]{1,0:T(8,128)(2,1)S(1)}, u32[]{:S(2)}, u32[]{:S(2)}) collective-permute-start(bf16[128,512]{1,0:T(8,128)(2,1)S(1)} %column.1.refs_0_), channel_id=1, source_target_pairs={{0,2},{1,3},{2,0},{3,1},{8,40},{9,41},{10,42},{11,43},{16,18},{17,... | collective-permute-start | bytes 393224 | tf_op jit(solution)/shard_map/ppermute | solution.py:171
  23.2 6.7 %collective-permute-start.1 = (bf16[128,512]{1,0:T(8,128)(2,1)S(1)}, bf16[128,512]{1,0:T(8,128)(2,1)S(1)}, u32[]{:S(2)}, u32[]{:S(2)}) collective-permute-start(bf16[128,512]{1,0:T(8,128)(2,1)S(1)} %column.1.refs_0_), channel_id=1, source_target_pairs={{0,1},{1,2},{2,3},{3,0},{8,24},{9,25},{10,26},{11,27},{16,17},{17,... | collective-permute-start | bytes 393224 | tf_op jit(solution)/shard_map/ppermute | solution.py:171
  29.9 14.0 %collective-permute-start.6 = (bf16[4,128,512]{2,1,0:T(8,128)(2,1)S(1)}, bf16[4,128,512]{2,1,0:T(8,128)(2,1)S(1)}, u32[]{:S(2)}, u32[]{:S(2)}) collective-permute-start(bf16[4,128,512]{2,1,0:T(8,128)(2,1)S(1)} %pack.1.after_ref.b0_ref), channel_id=1, source_target_pairs={{0,48},{1,49},{2,50},{3,51},{8,11},{9,8},{10,9},{11,10},{16,0},{17... | collective-permute-start | bytes 1572872 | tf_op jit(solution)/shard_map/ppermute | solution.py:171
  32.2 11.7 %collective-permute-start.5 = (bf16[4,128,512]{2,1,0:T(8,128)(2,1)S(1)}, bf16[4,128,512]{2,1,0:T(8,128)(2,1)S(1)}, u32[]{:S(2)}, u32[]{:S(2)}) collective-permute-start(bf16[4,128,512]{2,1,0:T(8,128)(2,1)S(1)} %pack.1.after_ref.b0_ref), channel_id=1, source_target_pairs={{0,32},{1,33},{2,34},{3,35},{8,10},{9,11},{10,8},{11,9},{16,48},{1... | collective-permute-start | bytes 1572872 | tf_op jit(solution)/shard_map/ppermute | solution.py:171
  32.7 14.9 %collective-permute-start.4 = (bf16[4,128,512]{2,1,0:T(8,128)(2,1)S(1)}, bf16[4,128,512]{2,1,0:T(8,128)(2,1)S(1)}, u32[]{:S(2)}, u32[]{:S(2)}) collective-permute-start(bf16[4,128,512]{2,1,0:T(8,128)(2,1)S(1)} %pack.1.after_ref.b0_ref), channel_id=1, source_target_pairs={{0,16},{1,17},{2,18},{3,19},{8,9},{9,10},{10,11},{11,8},{16,32},{1... | collective-permute-start | bytes 1572872 | tf_op jit(solution)/shard_map/ppermute | solution.py:171
  33.3 1.6 %copy-start = (bf16[2048,512]{1,0:T(8,128)(2,1)S(1)}, bf16[2048,512]{1,0:T(8,128)(2,1)}, u32[]{:S(2)}) copy-start(bf16[2048,512]{1,0:T(8,128)(2,1)} %wk_ref.1) | copy-start | bytes 6291460
  34.9 1.6 %copy-start.1 = (bf16[2048,512]{1,0:T(8,128)(2,1)S(1)}, bf16[2048,512]{1,0:T(8,128)(2,1)}, u32[]{:S(2)}) copy-start(bf16[2048,512]{1,0:T(8,128)(2,1)} %wv_ref.1) | copy-start | bytes 6291460
  49.0 5.3 %copy-start.2 = (bf16[256,512]{1,0:T(8,128)(2,1)S(1)}, bf16[256,512]{1,0:T(8,128)(2,1)}, u32[]{:S(2)}) copy-start(bf16[256,512]{1,0:T(8,128)(2,1)} %q_ref.1) | copy-start | bytes 786436
  49.0 5.3 %copy-start.3 = (bf16[256,512]{1,0:T(8,128)(2,1)S(1)}, bf16[256,512]{1,0:T(8,128)(2,1)}, u32[]{:S(2)}) copy-start(bf16[256,512]{1,0:T(8,128)(2,1)} %g_ref.1) | copy-start | bytes 786436
  49.0 5.3 %copy-start.5 = (s32[4]{0:T(128)S(1)}, s32[4]{0:T(128)}, u32[]{:S(2)}) copy-start(s32[4]{0:T(128)} %len_ref.1) | copy-start | bytes 52
  49.1 5.3 %collective-permute-start.7 = (f32[2,256,512]{2,1,0:T(8,128)S(1)}, f32[2,256,512]{2,1,0:T(8,128)S(1)}, u32[]{:S(2)}, u32[]{:S(2)}) collective-permute-start(f32[2,256,512]{2,1,0:T(8,128)S(1)} %project.3), channel_id=1, source_target_pairs={{0,8},{8,0},{1,9},{9,1},{2,10},{10,2},{3,11},{11,3},{4,12},{12,4},... | collective-permute-start | bytes 3145736 | tf_op jit(solution)/shard_map/ppermute | solution.py:157
  58.5 1.9 %collective-permute-start.8 = (bf16[2,256,512]{2,1,0:T(8,128)(2,1)S(1)}, bf16[2,256,512]{2,1,0:T(8,128)(2,1)S(1)}, u32[]{:S(2)}, u32[]{:S(2)}) collective-permute-start(bf16[2,256,512]{2,1,0:T(8,128)(2,1)S(1)} %get-tuple-element.22.mine_ref), channel_id=1, source_target_pairs={{0,8},{8,0},{1,9},{9,1},{2,10},{10,2},{3,11},{11,3},{4,12},{12,4},... | collective-permute-start | bytes 1572872 | tf_op jit(solution)/shard_map/ppermute | solution.py:157
  62.9 15.4 %collective-permute-start.9 = (bf16[4,128,512]{2,1,0:T(8,128)(2,1)S(1)}, bf16[4,128,512]{2,1,0:T(8,128)(2,1)S(1)}, u32[]{:S(2)}, u32[]{:S(2)}) collective-permute-start(bf16[4,128,512]{2,1,0:T(8,128)(2,1)S(1)} %get-tuple-element.24), channel_id=1, source_target_pairs={{0,16},{1,17},{2,18},{3,19},{8,9},{9,10},{10,11},{11,8},{16,32},{1... | collective-permute-start | bytes 1572872 | tf_op jit(solution)/shard_map/ppermute | solution.py:171
  63.2 15.1 %collective-permute-start.10 = (bf16[4,128,512]{2,1,0:T(8,128)(2,1)S(1)}, bf16[4,128,512]{2,1,0:T(8,128)(2,1)S(1)}, u32[]{:S(2)}, u32[]{:S(2)}) collective-permute-start(bf16[4,128,512]{2,1,0:T(8,128)(2,1)S(1)} %get-tuple-element.25), channel_id=1, source_target_pairs={{0,32},{1,33},{2,34},{3,35},{8,10},{9,11},{10,8},{11,9},{16,48},{1... | collective-permute-start | bytes 1572872 | tf_op jit(solution)/shard_map/ppermute | solution.py:171
  64.6 14.3 %collective-permute-start.11 = (bf16[4,128,512]{2,1,0:T(8,128)(2,1)S(1)}, bf16[4,128,512]{2,1,0:T(8,128)(2,1)S(1)}, u32[]{:S(2)}, u32[]{:S(2)}) collective-permute-start(bf16[4,128,512]{2,1,0:T(8,128)(2,1)S(1)} %get-tuple-element.26), channel_id=1, source_target_pairs={{0,48},{1,49},{2,50},{3,51},{8,11},{9,8},{10,9},{11,10},{16,0},{17... | collective-permute-start | bytes 1572872 | tf_op jit(solution)/shard_map/ppermute | solution.py:171
  79.2 6.8 %collective-permute-start.12 = (bf16[128,512]{1,0:T(8,128)(2,1)S(1)}, bf16[128,512]{1,0:T(8,128)(2,1)S(1)}, u32[]{:S(2)}, u32[]{:S(2)}) collective-permute-start(bf16[128,512]{1,0:T(8,128)(2,1)S(1)} %get-tuple-element.28), channel_id=1, source_target_pairs={{0,1},{1,2},{2,3},{3,0},{8,24},{9,25},{10,26},{11,27},{16,17},{17,... | collective-permute-start | bytes 393224 | tf_op jit(solution)/shard_map/ppermute | solution.py:171
  79.3 6.7 %collective-permute-start.13 = (bf16[128,512]{1,0:T(8,128)(2,1)S(1)}, bf16[128,512]{1,0:T(8,128)(2,1)S(1)}, u32[]{:S(2)}, u32[]{:S(2)}) collective-permute-start(bf16[128,512]{1,0:T(8,128)(2,1)S(1)} %get-tuple-element.29), channel_id=1, source_target_pairs={{0,2},{1,3},{2,0},{3,1},{8,40},{9,41},{10,42},{11,43},{16,18},{17,... | collective-permute-start | bytes 393224 | tf_op jit(solution)/shard_map/ppermute | solution.py:171
  80.8 5.8 %collective-permute-start.14 = (bf16[128,512]{1,0:T(8,128)(2,1)S(1)}, bf16[128,512]{1,0:T(8,128)(2,1)S(1)}, u32[]{:S(2)}, u32[]{:S(2)}) collective-permute-start(bf16[128,512]{1,0:T(8,128)(2,1)S(1)} %get-tuple-element.30), channel_id=1, source_target_pairs={{0,3},{1,0},{2,1},{3,2},{8,56},{9,57},{10,58},{11,59},{16,19},{17,... | collective-permute-start | bytes 393224 | tf_op jit(solution)/shard_map/ppermute | solution.py:171
  86.7 3.6 %collective-permute-start.15 = (bf16[4,16,512]{2,1,0:T(8,128)(2,1)S(1)}, bf16[4,16,512]{2,1,0:T(8,128)(2,1)S(1)}, u32[]{:S(2)}, u32[]{:S(2)}) collective-permute-start(bf16[4,16,512]{2,1,0:T(8,128)(2,1)S(1)} %get-tuple-element.32), channel_id=1, source_target_pairs={{0,8},{8,0},{1,9},{9,1},{2,10},{10,2},{3,11},{11,3},{4,12},{12,4},... | collective-permute-start | bytes 196616 | tf_op jit(solution)/shard_map/ppermute | solution.py:157

commit v4 on v3

--- a/solution.py
+++ b/solution.py
@@ -54,49 +54,70 @@
     )(*here, *blocks, wk, wv)
 
 
-def attend_kernel(pair_ref, len_ref, own_ref, got_ref, q_ref, g_ref, ctx_ref, gq_ref, grad_ref):
+def split(a):
+    low = lax.broadcasted_iota(jnp.int32, (128, 128), 1) < HDIM
+    a, zero = a.astype(F32), jnp.zeros((128, 128), F32)
+    return jnp.concatenate([jnp.where(low, a, zero), jnp.where(low, zero, a)], axis=0).astype(BF16)
+
+
+def attend_kernel(pair_ref, len_ref, own_ref, got_ref, q_ref, g_ref, grad_ref, kv_ref, pb_ref, ds_ref):
     scale = HDIM ** (-0.5)
-    low = lax.broadcasted_iota(jnp.int32, (128, 128), 1) < HDIM
     token = lax.broadcasted_iota(jnp.int32, (2, 128, 128), 1)
-    zero = jnp.zeros((128, 128), F32)
-
-    def split(a):
-        a = a.astype(F32)
-        return jnp.concatenate([jnp.where(low, a, zero), jnp.where(low, zero, a)], axis=0).astype(BF16)
-
     for i in range(2):
         valid = token < len_ref[pair_ref[0] * 2 + i]
         for p in range(4):
             at = (slice(128 * i, 128 * (i + 1)), slice(128 * p, 128 * (p + 1)))
-            ks = split((own_ref[0][at] + got_ref[0][at]).astype(BF16))
-            vs = split((own_ref[1][at] + got_ref[1][at]).astype(BF16))
+            k = (own_ref[0][at] + got_ref[0][at]).astype(BF16)
+            v = (own_ref[1][at] + got_ref[1][at]).astype(BF16)
+            kv_ref[(0, *at)], kv_ref[(1, *at)] = k, v
             q, g = q_ref[at], g_ref[at]
-            qs, gs = split(q), split(g)
-            s = nt(ks, q).reshape(2, 128, 128) * scale
+            s = nt(split(k), q).reshape(2, 128, 128) * scale
             s = jnp.where(valid, s, F32(-1e30))
             e = jnp.exp(s - jnp.max(s, axis=1, keepdims=True))
             prob = e / jnp.sum(e, axis=1, keepdims=True)
-            dp = nt(vs, g).reshape(2, 128, 128)
+            dp = nt(split(v), g).reshape(2, 128, 128)
             delta = jnp.sum(prob * dp, axis=1, keepdims=True)
             ds = (prob * (dp - delta) * scale).astype(BF16)
             pb = prob.astype(BF16)
-            ctx_ref[at] = nn(pb.reshape(256, 128).T, vs).astype(BF16)
-            gq_ref[at] = nn(ds.reshape(256, 128).T, ks).astype(BF16)
-            grad_ref[(0, *at)] = nn(jnp.concatenate([ds[0], ds[1]], axis=1), qs).astype(BF16)
-            grad_ref[(1, *at)] = nn(jnp.concatenate([pb[0], pb[1]], axis=1), gs).astype(BF16)
+            pb_ref[4 * i + p], ds_ref[4 * i + p] = pb.reshape(256, 128), ds.reshape(256, 128)
+            grad_ref[(0, *at)] = nn(jnp.concatenate([ds[0], ds[1]], axis=1), split(q)).astype(BF16)
+            grad_ref[(1, *at)] = nn(jnp.concatenate([pb[0], pb[1]], axis=1), split(g)).astype(BF16)
 
 
 def attend(pair, lengths, own, got, q, g):
-    one = jax.ShapeDtypeStruct((256, 512), BF16)
+    two = jax.ShapeDtypeStruct((2, 256, 512), BF16)
+    weights = jax.ShapeDtypeStruct((8, 256, 128), BF16)
     return pl.pallas_call(
         attend_kernel,
-        out_shape=(one, one, jax.ShapeDtypeStruct((2, 256, 512), BF16)),
+        out_shape=(two, two, weights, weights),
         in_specs=[SM, SM, VM, VM, VM, VM],
-        out_specs=(VM, VM, VM),
+        out_specs=(VM,) * 4,
         compiler_params=pltpu.CompilerParams(vmem_limit_bytes=20 << 20),
-        cost_estimate=pl.CostEstimate(flops=6 * 8 * 2 * 256 * 128 * 128, bytes_accessed=4 << 20, transcendentals=1 << 18),
+        cost_estimate=pl.CostEstimate(flops=4 * 8 * 2 * 256 * 128 * 128, bytes_accessed=4 << 20, transcendentals=1 << 18),
         name="attend",
     )(pair, lengths, own, got, q, g)
+
+
+def finish_kernel(kv_ref, pb_ref, ds_ref, ctx_ref, gq_ref, mark_ref):
+    mark_ref[...] = jnp.zeros((8, 128), F32)
+    for i in range(2):
+        for p in range(4):
+            at = (slice(128 * i, 128 * (i + 1)), slice(128 * p, 128 * (p + 1)))
+            ctx_ref[at] = nn(pb_ref[4 * i + p].T, split(kv_ref[(1, *at)])).astype(BF16)
+            gq_ref[at] = nn(ds_ref[4 * i + p].T, split(kv_ref[(0, *at)])).astype(BF16)
+
+
+def finish(kv, pb, ds):
+    one = jax.ShapeDtypeStruct((256, 512), BF16)
+    return pl.pallas_call(
+        finish_kernel,
+        out_shape=(one, one, jax.ShapeDtypeStruct((8, 128), F32)),
+        in_specs=[VM] * 3,
+        out_specs=(VM, VM, VM),
+        compiler_params=pltpu.CompilerParams(vmem_limit_bytes=12 << 20),
+        cost_estimate=pl.CostEstimate(flops=2 * 8 * 2 * 256 * 128 * 128, bytes_accessed=2 << 20, transcendentals=0),
+        name="finish",
+    )(kv, pb, ds)
 
 
 def stage_kernel(wk_ref, wv_ref, after_ref, k_ref, v_ref, sems):
@@ -124,33 +145,30 @@
     )(wk, wv, after)
 
 
-def back_kernel(core_ref, y_ref, x_ref, mine_ref, theirs_ref, wk_ref, wv_ref, o0_ref, o1_ref, o2_ref, o3_ref, all_ref):
-    for side, ref in enumerate((mine_ref, theirs_ref)):
-        pair = core_ref[0] if side == 0 else 1 - core_ref[0]
-        for x in range(NX):
-            at = slice(512 * x, 512 * (x + 1))
-            r = (nt(ref[0], wk_ref[at]) + nt(ref[1], wv_ref[at])).astype(BF16)
-            for i in range(2):
-                start = pl.multiple_of(pair * 64 + 32 * i, 32)
-                all_ref[:, x, pl.ds(start, 32), :] = r[128 * i : 128 * (i + 1)].reshape(NY, 32, 512)
+def back_kernel(core_ref, y_ref, x_ref, grad_ref, wk_ref, wv_ref, o0_ref, o1_ref, o2_ref, o3_ref, all_ref):
+    for x in range(NX):
+        at = slice(512 * x, 512 * (x + 1))
+        r = (nt(grad_ref[0], wk_ref[at]) + nt(grad_ref[1], wv_ref[at])).astype(BF16)
+        for i in range(2):
+            all_ref[:, x, 32 * i : 32 * (i + 1), :] = r[128 * i : 128 * (i + 1)].reshape(NY, 32, 512)
     for far, ref in enumerate((o0_ref, o1_ref, o2_ref, o3_ref)):
         for near in range(4):
             y, x = place(core_ref[0], y_ref[0], x_ref[0], far, near)
             ref[near] = all_ref[y, x]
 
 
-def back(here, mine, theirs, wk, wv):
-    part = jax.ShapeDtypeStruct((4, 128, 512), BF16)
+def back(here, grads, wk, wv):
+    part = jax.ShapeDtypeStruct((4, 64, 512), BF16)
     return pl.pallas_call(
         back_kernel,
-        out_shape=(part, part, part, part),
-        in_specs=[SM] * 3 + [VM] * 4,
-        out_specs=(VM, VM, VM, VM),
-        scratch_shapes=[pltpu.VMEM((NY, NX, 128, 512), BF16)],
+        out_shape=(part,) * 4,
+        in_specs=[SM] * 3 + [VM] * 3,
+        out_specs=(VM,) * 4,
+        scratch_shapes=[pltpu.VMEM((NY, NX, 64, 512), BF16)],
         compiler_params=pltpu.CompilerParams(vmem_limit_bytes=20 << 20),
-        cost_estimate=pl.CostEstimate(flops=2 * 2 * 512 * 2048 * 512, bytes_accessed=7 << 20, transcendentals=0),
+        cost_estimate=pl.CostEstimate(flops=2 * 2 * 256 * 2048 * 512, bytes_accessed=6 << 20, transcendentals=0),
         name="back",
-    )(*here, mine, theirs, wk, wv)
+    )(*here, grads, wk, wv)
 
 
 def swap(block):
@@ -223,23 +241,27 @@
     return [blocks, *shifted(1, [blocks] * 3)]
 
 
-def total_kernel(p0_ref, p1_ref, p2_ref, p3_ref, *out_refs):
-    for near, ref in enumerate(out_refs):
-        total = p0_ref[near].astype(F32) + p1_ref[near].astype(F32)
-        ref[...] = (total + p2_ref[near].astype(F32) + p3_ref[near].astype(F32)).astype(BF16)
-
-
-def total(parts):
+def total_kernel(core_ref, after_ref, *refs):
+    for side in range(2):
+        base = 64 * (core_ref[0] if side == 0 else 1 - core_ref[0])
+        p0_ref, p1_ref, p2_ref, p3_ref = refs[4 * side : 4 * side + 4]
+        for near in range(4):
+            total = p0_ref[near].astype(F32) + p1_ref[near].astype(F32)
+            total = (total + p2_ref[near].astype(F32) + p3_ref[near].astype(F32)).astype(BF16)
+            refs[8 + near][pl.ds(pl.multiple_of(base, 64), 64), :] = total
+
+
+def total(core, after, mine, theirs):
     one = jax.ShapeDtypeStruct((128, 512), BF16)
     return pl.pallas_call(
         total_kernel,
         out_shape=(one, one, one, one),
-        in_specs=[VM] * 4,
+        in_specs=[SM] + [VM] * 9,
         out_specs=(VM,) * 4,
         compiler_params=pltpu.CompilerParams(vmem_limit_bytes=8 << 20),
         cost_estimate=pl.CostEstimate(flops=1 << 20, bytes_accessed=5 << 19, transcendentals=0),
         name="total",
-    )(*parts)
+    )(core, after, *mine, *theirs)
 
 
 def fold_kernel(core_ref, p0_ref, p1_ref, p2_ref, p3_ref, keep_ref, send_ref):
@@ -265,8 +287,8 @@
     )(core, *parts)
 
 
-def scatter(parts, core):
-    line = total([parts[0], *shifted(1, parts[1:])])
+def scatter(mine, theirs, core, after):
+    line = total(core, after, mine, theirs)
     keep, send = fold(core, [line[0], *shifted(0, line[1:])])
     ring = small(join_kernel, "join", (NZ, NH, 16, 512), core, keep, swap(send))
     ring = lax.all_to_all(ring.reshape(NZ * NH, 16, 512), ("zl", "zh"), 0, 0)
@@ -278,12 +300,15 @@
     core = here[0]
     blocks = gather(memory, core)
     key_weight, value_weight = stage(key_weight, value_weight, blocks[0])
-    other = project(True, here, blocks, key_weight, value_weight)
-    got = swap(other)
+    got = swap(project(True, here, blocks, key_weight, value_weight))
     own = project(False, here, blocks, key_weight, value_weight)
-    ctx, gq, mine = attend(core, memory_lengths, own, got, queries, grad_context)
-    parts = back(here, mine, swap(mine), key_weight, value_weight)
-    return ctx, gq, scatter(parts, core)
+    grads, kv, pb, ds = attend(core, memory_lengths, own, got, queries, grad_context)
+    mine = back(here, grads, key_weight, value_weight)
+    mine = [mine[0], *shifted(1, mine[1:])]
+    theirs = back(here, swap(grads), key_weight, value_weight)
+    theirs = [theirs[0], *shifted(1, theirs[1:])]
+    ctx, gq, mark = finish(kv, pb, ds)
+    return ctx, gq, scatter(mine, theirs, core, mark)
 
 
 def solution(mesh):

time: 101 us -> 96.6 us (0.956)
  waiting for transfers between devices: 38.8 us -> 32.1 us
  starting transfers between devices: 21.2 us -> 23.4 us
    ppermute x12 -> x15, waiting for transfers between devices: 34.6 us -> 29.4 us  [shifted(): lax.ppermute(b, ('y', 'core', 'x'), route(along, k))]
    ppermute x12 -> x15, starting transfers between devices: 12.9 us -> 15.3 us  [shifted(): lax.ppermute(b, ('y', 'core', 'x'), route(along, k))]
    ppermute x4, waiting for transfers between devices: 4.25 us -> 2.72 us  [swap(): return lax.ppermute(block, 'core', [(0, 1), (1, 0)])]
    pallas_call x3 -> x5, Pallas kernels: 6.93 us -> 7.15 us  [the longest x1 2.86 us: attend(): pl.pallas_call(attend_kernel, out_shape=(two, two, weights, weights), in_...]
  transfers between devices with their start and end apart: 16 -> 19, of which waited for: 13 -> 13; matrix products, arithmetic and copies ran while one was open for 0% -> 0% of each run, Pallas kernels for 2% -> 6%
where the time goes in v4:
time: 96.6 us; the launch traced here: 96.1 us
  waiting for transfers between devices  32.1 us (33%)
  blocking collectives  25 us (26%)
  starting transfers between devices  23.4 us (24%)
  Pallas kernels  10.3 us (11%)
  local copies, waits for them, and re-layouts  3.91 us (4%)
    ppermute x15, waiting for transfers between devices, shifted(): lax.ppermute(b, ('y', 'core', 'x'), route(along, k))  29.4 us
    all_to_all x1, blocking collectives, gather(): ring = lax.all_to_all(copies, ('zl', 'zh'), 0, 0).reshape(NZ, NH, 16, 512)  15.6 us
    ppermute x15, starting transfers between devices, shifted(): lax.ppermute(b, ('y', 'core', 'x'), route(along, k))  15.3 us
    all_to_all x1, blocking collectives, scatter(): ring = lax.all_to_all(ring.reshape(NZ * NH, 16, 512), ('zl', 'zh'), 0, 0)  9.34 us
    ppermute x4, starting transfers between devices, swap(): return lax.ppermute(block, 'core', [(0, 1), (1, 0)])  8.09 us
    unnamed x12, local copies, waits for them, and re-layouts  3.91 us
    pallas_call x1, Pallas kernels, attend(): pl.pallas_call(attend_kernel, out_shape=(two, two, weights, weights), in_...  2.86 us
    pallas_call x2, Pallas kernels, back(): pl.pallas_call(back_kernel, out_shape=(part,) * 4, in_specs=[SM] * 3 + [V...  2.76 us
  transfers between devices with their start and end apart: 19, of which 13 were waited for; matrix products, arithmetic and copies ran while one was open for 0% of the time, Pallas kernels for 6%

profile of v4, /device:TPU:1, one launch (start us, length us, event | category | flops | bytes accessed | tf_op | source)
XLA Modules:
  0.0 96.1 jit_solution(1251685417127207686)
XLA Ops:
  0.6 0.7 copy-done.4
  1.4 15.6 %all_to_all.10 = bf16[8,16,512]{2,1,0:T(8,128)(2,1)S(1)} all-to-all(bf16[8,16,512]{2,1,0:T(8,128)(2,1)S(1)} %spread.1), channel_id=1, replica_groups=mesh['zl'=4,'y'=4,'core'=2,'zh'=2,'x'=4] {'zl','zh'}, dimensions={0} | all-to-all | bytes 262144 | tf_op jit(solution)/shard_map/all_to_all | solution.py:237
  17.0 2.2 %collective-permute-start = (bf16[4,16,512]{2,1,0:T(8,128)(2,1)S(1)}, bf16[4,16,512]{2,1,0:T(8,128)(2,1)S(1)}, u32[]{:S(2)}, u32[]{:S(2)}) collective-permute-start(bf16[4,16,512]{2,1,0:T(8,128)(2,1)S(1)} %pick.1), channel_id=1, source_target_pairs={{0,8},{8,0},{1,9},{9,1},{2,10},{10,2},{3,11},{11,3},{4,12},{12,4},... | collective-permute-start | bytes 196616 | tf_op jit(solution)/shard_map/ppermute | solution.py:175
  19.1 0.9 collective-permute-done.got_ref
  20.1 2.8 %collective-permute-start.3 = (bf16[128,512]{1,0:T(8,128)(2,1)S(1)}, bf16[128,512]{1,0:T(8,128)(2,1)S(1)}, u32[]{:S(2)}, u32[]{:S(2)}) collective-permute-start(bf16[128,512]{1,0:T(8,128)(2,1)S(1)} %column.1.refs_0_), channel_id=1, source_target_pairs={{0,3},{1,0},{2,1},{3,2},{8,56},{9,57},{10,58},{11,59},{16,19},{17,... | collective-permute-start | bytes 393224 | tf_op jit(solution)/shard_map/ppermute | solution.py:189
  23.9 2.3 %collective-permute-done.3.refs_3_ = bf16[128,512]{1,0:T(8,128)(2,1)S(1)} collective-permute-done((bf16[128,512]{1,0:T(8,128)(2,1)S(1)}, bf16[128,512]{1,0:T(8,128)(2,1)S(1)}, u32[]{:S(2)}, u32[]{:S(2)}) %collective-permute-start.3) | collective-permute-done | bytes 131104 | tf_op jit(solution)/shard_map/ppermute | solution.py:189
  26.2 2.3 %collective-permute-done.2.refs_2_ = bf16[128,512]{1,0:T(8,128)(2,1)S(1)} collective-permute-done((bf16[128,512]{1,0:T(8,128)(2,1)S(1)}, bf16[128,512]{1,0:T(8,128)(2,1)S(1)}, u32[]{:S(2)}, u32[]{:S(2)}) %collective-permute-start.2) | collective-permute-done | bytes 131104 | tf_op jit(solution)/shard_map/ppermute | solution.py:189
  28.5 1.4 %collective-permute-done.1.refs_1_ = bf16[128,512]{1,0:T(8,128)(2,1)S(1)} collective-permute-done((bf16[128,512]{1,0:T(8,128)(2,1)S(1)}, bf16[128,512]{1,0:T(8,128)(2,1)S(1)}, u32[]{:S(2)}, u32[]{:S(2)}) %collective-permute-start.1) | collective-permute-done | bytes 131104 | tf_op jit(solution)/shard_map/ppermute | solution.py:189
  29.9 2.3 %collective-permute-start.6 = (bf16[4,128,512]{2,1,0:T(8,128)(2,1)S(1)}, bf16[4,128,512]{2,1,0:T(8,128)(2,1)S(1)}, u32[]{:S(2)}, u32[]{:S(2)}) collective-permute-start(bf16[4,128,512]{2,1,0:T(8,128)(2,1)S(1)} %pack.1.after_ref.b0_ref), channel_id=1, source_target_pairs={{0,48},{1,49},{2,50},{3,51},{8,11},{9,8},{10,9},{11,10},{16,0},{17... | collective-permute-start | bytes 1572872 | tf_op jit(solution)/shard_map/ppermute | solution.py:189
  33.3 1.6 %copy-done = bf16[2048,512]{1,0:T(8,128)(2,1)S(1)} copy-done((bf16[2048,512]{1,0:T(8,128)(2,1)S(1)}, bf16[2048,512]{1,0:T(8,128)(2,1)}, u32[]{:S(2)}) %copy-start) | copy-done | bytes 2097176
  34.9 1.6 %copy-done.1 = bf16[2048,512]{1,0:T(8,128)(2,1)S(1)} copy-done((bf16[2048,512]{1,0:T(8,128)(2,1)S(1)}, bf16[2048,512]{1,0:T(8,128)(2,1)}, u32[]{:S(2)}) %copy-start.1) | copy-done | bytes 2097176
  36.8 7.1 %collective-permute-done.6.b3_ref = bf16[4,128,512]{2,1,0:T(8,128)(2,1)S(1)} collective-permute-done((bf16[4,128,512]{2,1,0:T(8,128)(2,1)S(1)}, bf16[4,128,512]{2,1,0:T(8,128)(2,1)S(1)}, u32[]{:S(2)}, u32[]{:S(2)}) %collective-permute-start.6) | collective-permute-done | bytes 524320 | tf_op jit(solution)/shard_map/ppermute | solution.py:189
  43.9 3.7 %collective-permute-done.4.b1_ref = bf16[4,128,512]{2,1,0:T(8,128)(2,1)S(1)} collective-permute-done((bf16[4,128,512]{2,1,0:T(8,128)(2,1)S(1)}, bf16[4,128,512]{2,1,0:T(8,128)(2,1)S(1)}, u32[]{:S(2)}, u32[]{:S(2)}) %collective-permute-start.4) | collective-permute-done | bytes 524320 | tf_op jit(solution)/shard_map/ppermute | solution.py:189
  47.6 1.4 %project.3 = f32[2,256,512]{2,1,0:T(8,128)S(1)} custom-call(s32[1]{0:T(128)} %bitcast.core_ref.pair_ref, s32[1]{0:T(128)} %bitcast.1.y_ref, s32[1]{0:T(128)} %bitcast.2.x_ref, bf16[4,128,512]{2,1,0:T(8,128)(2,1)S(1)} %pack.1.after_ref.b0_ref, bf16[4,128,512]{2,1,0:T(8,128)(2,1)S(1)} %collective-permute-done.4.b1_ref, ...), custom_call_target="tpu_custom_call" | custom-call | flops 1073741824 | bytes 7340032 | tf_op jit(solution)/shard_map/project/pallas_call | solution.py:45
  49.1 3.0 %collective-permute-start.7 = (f32[2,256,512]{2,1,0:T(8,128)S(1)}, f32[2,256,512]{2,1,0:T(8,128)S(1)}, u32[]{:S(2)}, u32[]{:S(2)}) collective-permute-start(f32[2,256,512]{2,1,0:T(8,128)S(1)} %project.3), channel_id=1, source_target_pairs={{0,8},{8,0},{1,9},{9,1},{2,10},{10,2},{3,11},{11,3},{4,12},{12,4},... | collective-permute-start | bytes 3145736 | tf_op jit(solution)/shard_map/ppermute | solution.py:175
  52.1 1.4 %project.2.own_ref = f32[2,256,512]{2,1,0:T(8,128)S(1)} custom-call(s32[1]{0:T(128)} %bitcast.core_ref.pair_ref, s32[1]{0:T(128)} %bitcast.1.y_ref, s32[1]{0:T(128)} %bitcast.2.x_ref, bf16[4,128,512]{2,1,0:T(8,128)(2,1)S(1)} %pack.1.after_ref.b0_ref, bf16[4,128,512]{2,1,0:T(8,128)(2,1)S(1)} %collective-permute-done.4.b1_ref, ...), custom_call_target="tpu_custom_call" | custom-call | flops 1073741824 | bytes 7340032 | tf_op jit(solution)/shard_map/project/pallas_call | solution.py:45
  53.4 0.9 collective-permute-done.7.got_ref
  54.4 2.9 %attend.1 = (bf16[2,256,512]{2,1,0:T(8,128)(2,1)S(1)}, bf16[2,256,512]{2,1,0:T(8,128)(2,1)S(1)}, bf16[8,256,128]{2,1,0:T(8,128)(2,1)S(1)}, bf16[8,256,128]{2,1,0:T(8,128)(2,1)S(1)}) custom-call(s32[1]{0:T(128)} %bitcast.core_ref.pair_ref, s32[4]{0:T(128)S(1)} %copy-done.5, f32[2,256,512]{2,1,0:T(8,128)S(1)} %project.2.own_ref, ...), custom_call_target="tpu_custom_call" | custom-call | flops 268435456 | bytes 4194304 | tf_op jit(solution)/shard_map/attend/pallas_call | solution.py:90
  57.7 1.4 %back.2 = (bf16[4,64,512]{2,1,0:T(8,128)(2,1)S(1)}, bf16[4,64,512]{2,1,0:T(8,128)(2,1)S(1)}, bf16[4,64,512]{2,1,0:T(8,128)(2,1)S(1)}, bf16[4,64,512]{2,1,0:T(8,128)(2,1)S(1)}) custom-call(s32[1]{0:T(128)} %bitcast.core_ref.pair_ref, s32[1]{0:T(128)} %bitcast.1.y_ref, s32[1]{0:T(128)} %bitcast.2.x_ref, bf16[2,256,512]{2,1,0:T(8,128)(2,1)S(1)} %get-tuple-element.34.grad_ref, ...), custom_call_target="tpu_custom_call" | custom-call | flops 1073741824 | bytes 6291456 | tf_op jit(solution)/shard_map/back/pallas_call | solution.py:162
  59.2 1.5 %collective-permute-start.9 = (bf16[4,64,512]{2,1,0:T(8,128)(2,1)S(1)}, bf16[4,64,512]{2,1,0:T(8,128)(2,1)S(1)}, u32[]{:S(2)}, u32[]{:S(2)}) collective-permute-start(bf16[4,64,512]{2,1,0:T(8,128)(2,1)S(1)} %get-tuple-element.37), channel_id=1, source_target_pairs={{0,32},{1,33},{2,34},{3,35},{8,10},{9,11},{10,8},{11,9},{16,48},{1... | collective-permute-start | bytes 786440 | tf_op jit(solution)/shard_map/ppermute | solution.py:189
  60.6 1.2 %collective-permute-start.10 = (bf16[4,64,512]{2,1,0:T(8,128)(2,1)S(1)}, bf16[4,64,512]{2,1,0:T(8,128)(2,1)S(1)}, u32[]{:S(2)}, u32[]{:S(2)}) collective-permute-start(bf16[4,64,512]{2,1,0:T(8,128)(2,1)S(1)} %get-tuple-element.38), channel_id=1, source_target_pairs={{0,48},{1,49},{2,50},{3,51},{8,11},{9,8},{10,9},{11,10},{16,0},{17... | collective-permute-start | bytes 786440 | tf_op jit(solution)/shard_map/ppermute | solution.py:189
  61.8 1.4 %back.3 = (bf16[4,64,512]{2,1,0:T(8,128)(2,1)S(1)}, bf16[4,64,512]{2,1,0:T(8,128)(2,1)S(1)}, bf16[4,64,512]{2,1,0:T(8,128)(2,1)S(1)}, bf16[4,64,512]{2,1,0:T(8,128)(2,1)S(1)}) custom-call(s32[1]{0:T(128)} %bitcast.core_ref.pair_ref, s32[1]{0:T(128)} %bitcast.1.y_ref, s32[1]{0:T(128)} %bitcast.2.x_ref, ...), custom_call_target="tpu_custom_call" | custom-call | flops 1073741824 | bytes 6291456 | tf_op jit(solution)/shard_map/back/pallas_call | solution.py:162
  63.9 1.9 %collective-permute-start.13 = (bf16[4,64,512]{2,1,0:T(8,128)(2,1)S(1)}, bf16[4,64,512]{2,1,0:T(8,128)(2,1)S(1)}, u32[]{:S(2)}, u32[]{:S(2)}) collective-permute-start(bf16[4,64,512]{2,1,0:T(8,128)(2,1)S(1)} %get-tuple-element.41), channel_id=1, source_target_pairs={{0,32},{1,33},{2,34},{3,35},{8,10},{9,11},{10,8},{11,9},{16,48},{1... | collective-permute-start | bytes 786440 | tf_op jit(solution)/shard_map/ppermute | solution.py:189
  65.8 2.9 %collective-permute-done.8.refs_1_ = bf16[4,64,512]{2,1,0:T(8,128)(2,1)S(1)} collective-permute-done((bf16[4,64,512]{2,1,0:T(8,128)(2,1)S(1)}, bf16[4,64,512]{2,1,0:T(8,128)(2,1)S(1)}, u32[]{:S(2)}, u32[]{:S(2)}) %collective-permute-start.8) | collective-permute-done | bytes 262176 | tf_op jit(solution)/shard_map/ppermute | solution.py:189
  68.7 1.3 %finish.1 = (bf16[256,512]{1,0:T(8,128)(2,1)}, bf16[256,512]{1,0:T(8,128)(2,1)}, f32[8,128]{1,0:T(8,128)S(1)}) custom-call(bf16[2,256,512]{2,1,0:T(8,128)(2,1)S(1)} %get-tuple-element.28.kv_ref, bf16[8,256,128]{2,1,0:T(8,128)(2,1)S(1)} %get-tuple-element.29.pb_ref, bf16[8,256,128]{2,1,0:T(8,128)(2,1)S(1)} %get-tuple-element.30.ds_ref), custom_call_target="tpu_custom_call" | custom-call | flops 134217728 | bytes 2097152 | tf_op jit(solution)/shard_map/finish/pallas_call | solution.py:112
  70.0 4.3 %collective-permute-done.12.refs_5_ = bf16[4,64,512]{2,1,0:T(8,128)(2,1)S(1)} collective-permute-done((bf16[4,64,512]{2,1,0:T(8,128)(2,1)S(1)}, bf16[4,64,512]{2,1,0:T(8,128)(2,1)S(1)}, u32[]{:S(2)}, u32[]{:S(2)}) %collective-permute-start.12) | collective-permute-done | bytes 262176 | tf_op jit(solution)/shard_map/ppermute | solution.py:189
  75.3 1.5 %collective-permute-start.16 = (bf16[128,512]{1,0:T(8,128)(2,1)S(1)}, bf16[128,512]{1,0:T(8,128)(2,1)S(1)}, u32[]{:S(2)}, u32[]{:S(2)}) collective-permute-start(bf16[128,512]{1,0:T(8,128)(2,1)S(1)} %get-tuple-element.45), channel_id=1, source_target_pairs={{0,2},{1,3},{2,0},{3,1},{8,40},{9,41},{10,42},{11,43},{16,18},{17,... | collective-permute-start | bytes 393224 | tf_op jit(solution)/shard_map/ppermute | solution.py:189
  76.8 1.2 %collective-permute-start.17 = (bf16[128,512]{1,0:T(8,128)(2,1)S(1)}, bf16[128,512]{1,0:T(8,128)(2,1)S(1)}, u32[]{:S(2)}, u32[]{:S(2)}) collective-permute-start(bf16[128,512]{1,0:T(8,128)(2,1)S(1)} %get-tuple-element.46), channel_id=1, source_target_pairs={{0,3},{1,0},{2,1},{3,2},{8,56},{9,57},{10,58},{11,59},{16,19},{17,... | collective-permute-start | bytes 393224 | tf_op jit(solution)/shard_map/ppermute | solution.py:189
  78.0 4.0 %collective-permute-done.15.p1_ref = bf16[128,512]{1,0:T(8,128)(2,1)S(1)} collective-permute-done((bf16[128,512]{1,0:T(8,128)(2,1)S(1)}, bf16[128,512]{1,0:T(8,128)(2,1)S(1)}, u32[]{:S(2)}, u32[]{:S(2)}) %collective-permute-start.15) | collective-permute-done | bytes 131104 | tf_op jit(solution)/shard_map/ppermute | solution.py:189
  82.7 2.5 %collective-permute-start.18 = (bf16[4,16,512]{2,1,0:T(8,128)(2,1)S(1)}, bf16[4,16,512]{2,1,0:T(8,128)(2,1)S(1)}, u32[]{:S(2)}, u32[]{:S(2)}) collective-permute-start(bf16[4,16,512]{2,1,0:T(8,128)(2,1)S(1)} %get-tuple-element.48), channel_id=1, source_target_pairs={{0,8},{8,0},{1,9},{9,1},{2,10},{10,2},{3,11},{11,3},{4,12},{12,4},... | collective-permute-start | bytes 196616 | tf_op jit(solution)/shard_map/ppermute | solution.py:175
  85.2 0.9 collective-permute-done.18.got_ref
  86.1 9.3 %all_to_all.11 = bf16[8,16,512]{2,1,0:T(8,128)(2,1)S(1)} all-to-all(bf16[8,16,512]{2,1,0:T(8,128)(2,1)S(1)} %bitcast.7), channel_id=1, replica_groups=mesh['zl'=4,'y'=4,'core'=2,'zh'=2,'x'=4] {'zl','zh'}, dimensions={0} | all-to-all | bytes 262144 | tf_op jit(solution)/shard_map/all_to_all | solution.py:294
  (35 shorter events, 6.1 us)
Async XLA Ops:
  0.6 0.7 copy-start.4
  17.0 3.1 %collective-permute-start = (bf16[4,16,512]{2,1,0:T(8,128)(2,1)S(1)}, bf16[4,16,512]{2,1,0:T(8,128)(2,1)S(1)}, u32[]{:S(2)}, u32[]{:S(2)}) collective-permute-start(bf16[4,16,512]{2,1,0:T(8,128)(2,1)S(1)} %pick.1), channel_id=1, source_target_pairs={{0,8},{8,0},{1,9},{9,1},{2,10},{10,2},{3,11},{11,3},{4,12},{12,4},... | collective-permute-start | bytes 196616 | tf_op jit(solution)/shard_map/ppermute | solution.py:175
  20.1 6.1 %collective-permute-start.3 = (bf16[128,512]{1,0:T(8,128)(2,1)S(1)}, bf16[128,512]{1,0:T(8,128)(2,1)S(1)}, u32[]{:S(2)}, u32[]{:S(2)}) collective-permute-start(bf16[128,512]{1,0:T(8,128)(2,1)S(1)} %column.1.refs_0_), channel_id=1, source_target_pairs={{0,3},{1,0},{2,1},{3,2},{8,56},{9,57},{10,58},{11,59},{16,19},{17,... | collective-permute-start | bytes 393224 | tf_op jit(solution)/shard_map/ppermute | solution.py:189
  22.9 5.6 %collective-permute-start.2 = (bf16[128,512]{1,0:T(8,128)(2,1)S(1)}, bf16[128,512]{1,0:T(8,128)(2,1)S(1)}, u32[]{:S(2)}, u32[]{:S(2)}) collective-permute-start(bf16[128,512]{1,0:T(8,128)(2,1)S(1)} %column.1.refs_0_), channel_id=1, source_target_pairs={{0,2},{1,3},{2,0},{3,1},{8,40},{9,41},{10,42},{11,43},{16,18},{17,... | collective-permute-start | bytes 393224 | tf_op jit(solution)/shard_map/ppermute | solution.py:189
  23.2 6.7 %collective-permute-start.1 = (bf16[128,512]{1,0:T(8,128)(2,1)S(1)}, bf16[128,512]{1,0:T(8,128)(2,1)S(1)}, u32[]{:S(2)}, u32[]{:S(2)}) collective-permute-start(bf16[128,512]{1,0:T(8,128)(2,1)S(1)} %column.1.refs_0_), channel_id=1, source_target_pairs={{0,1},{1,2},{2,3},{3,0},{8,24},{9,25},{10,26},{11,27},{16,17},{17,... | collective-permute-start | bytes 393224 | tf_op jit(solution)/shard_map/ppermute | solution.py:189
  29.9 14.0 %collective-permute-start.6 = (bf16[4,128,512]{2,1,0:T(8,128)(2,1)S(1)}, bf16[4,128,512]{2,1,0:T(8,128)(2,1)S(1)}, u32[]{:S(2)}, u32[]{:S(2)}) collective-permute-start(bf16[4,128,512]{2,1,0:T(8,128)(2,1)S(1)} %pack.1.after_ref.b0_ref), channel_id=1, source_target_pairs={{0,48},{1,49},{2,50},{3,51},{8,11},{9,8},{10,9},{11,10},{16,0},{17... | collective-permute-start | bytes 1572872 | tf_op jit(solution)/shard_map/ppermute | solution.py:189
  32.2 11.7 %collective-permute-start.5 = (bf16[4,128,512]{2,1,0:T(8,128)(2,1)S(1)}, bf16[4,128,512]{2,1,0:T(8,128)(2,1)S(1)}, u32[]{:S(2)}, u32[]{:S(2)}) collective-permute-start(bf16[4,128,512]{2,1,0:T(8,128)(2,1)S(1)} %pack.1.after_ref.b0_ref), channel_id=1, source_target_pairs={{0,32},{1,33},{2,34},{3,35},{8,10},{9,11},{10,8},{11,9},{16,48},{1... | collective-permute-start | bytes 1572872 | tf_op jit(solution)/shard_map/ppermute | solution.py:189
  32.7 14.9 %collective-permute-start.4 = (bf16[4,128,512]{2,1,0:T(8,128)(2,1)S(1)}, bf16[4,128,512]{2,1,0:T(8,128)(2,1)S(1)}, u32[]{:S(2)}, u32[]{:S(2)}) collective-permute-start(bf16[4,128,512]{2,1,0:T(8,128)(2,1)S(1)} %pack.1.after_ref.b0_ref), channel_id=1, source_target_pairs={{0,16},{1,17},{2,18},{3,19},{8,9},{9,10},{10,11},{11,8},{16,32},{1... | collective-permute-start | bytes 1572872 | tf_op jit(solution)/shard_map/ppermute | solution.py:189
  33.3 1.6 %copy-start = (bf16[2048,512]{1,0:T(8,128)(2,1)S(1)}, bf16[2048,512]{1,0:T(8,128)(2,1)}, u32[]{:S(2)}) copy-start(bf16[2048,512]{1,0:T(8,128)(2,1)} %wk_ref.1) | copy-start | bytes 6291460
  34.9 1.6 %copy-start.1 = (bf16[2048,512]{1,0:T(8,128)(2,1)S(1)}, bf16[2048,512]{1,0:T(8,128)(2,1)}, u32[]{:S(2)}) copy-start(bf16[2048,512]{1,0:T(8,128)(2,1)} %wv_ref.1) | copy-start | bytes 6291460
  49.0 5.3 %copy-start.2 = (bf16[256,512]{1,0:T(8,128)(2,1)S(1)}, bf16[256,512]{1,0:T(8,128)(2,1)}, u32[]{:S(2)}) copy-start(bf16[256,512]{1,0:T(8,128)(2,1)} %q_ref.1) | copy-start | bytes 786436
  49.0 5.3 %copy-start.3 = (bf16[256,512]{1,0:T(8,128)(2,1)S(1)}, bf16[256,512]{1,0:T(8,128)(2,1)}, u32[]{:S(2)}) copy-start(bf16[256,512]{1,0:T(8,128)(2,1)} %g_ref.1) | copy-start | bytes 786436
  49.0 5.3 %copy-start.5 = (s32[4]{0:T(128)S(1)}, s32[4]{0:T(128)}, u32[]{:S(2)}) copy-start(s32[4]{0:T(128)} %len_ref.1) | copy-start | bytes 52
  49.1 5.3 %collective-permute-start.7 = (f32[2,256,512]{2,1,0:T(8,128)S(1)}, f32[2,256,512]{2,1,0:T(8,128)S(1)}, u32[]{:S(2)}, u32[]{:S(2)}) collective-permute-start(f32[2,256,512]{2,1,0:T(8,128)S(1)} %project.3), channel_id=1, source_target_pairs={{0,8},{8,0},{1,9},{9,1},{2,10},{10,2},{3,11},{11,3},{4,12},{12,4},... | collective-permute-start | bytes 3145736 | tf_op jit(solution)/shard_map/ppermute | solution.py:175
  57.2 4.6 %collective-permute-start.11 = (bf16[2,256,512]{2,1,0:T(8,128)(2,1)S(1)}, bf16[2,256,512]{2,1,0:T(8,128)(2,1)S(1)}, u32[]{:S(2)}, u32[]{:S(2)}) collective-permute-start(bf16[2,256,512]{2,1,0:T(8,128)(2,1)S(1)} %get-tuple-element.34.grad_ref), channel_id=1, source_target_pairs={{0,8},{8,0},{1,9},{9,1},{2,10},{10,2},{3,11},{11,3},{4,12},{12,4},... | collective-permute-start | bytes 1572872 | tf_op jit(solution)/shard_map/ppermute | solution.py:175
  59.1 9.6 %collective-permute-start.8 = (bf16[4,64,512]{2,1,0:T(8,128)(2,1)S(1)}, bf16[4,64,512]{2,1,0:T(8,128)(2,1)S(1)}, u32[]{:S(2)}, u32[]{:S(2)}) collective-permute-start(bf16[4,64,512]{2,1,0:T(8,128)(2,1)S(1)} %get-tuple-element.36), channel_id=1, source_target_pairs={{0,16},{1,17},{2,18},{3,19},{8,9},{9,10},{10,11},{11,8},{16,32},{1... | collective-permute-start | bytes 786440 | tf_op jit(solution)/shard_map/ppermute | solution.py:189
  59.2 10.8 %collective-permute-start.9 = (bf16[4,64,512]{2,1,0:T(8,128)(2,1)S(1)}, bf16[4,64,512]{2,1,0:T(8,128)(2,1)S(1)}, u32[]{:S(2)}, u32[]{:S(2)}) collective-permute-start(bf16[4,64,512]{2,1,0:T(8,128)(2,1)S(1)} %get-tuple-element.37), channel_id=1, source_target_pairs={{0,32},{1,33},{2,34},{3,35},{8,10},{9,11},{10,8},{11,9},{16,48},{1... | collective-permute-start | bytes 786440 | tf_op jit(solution)/shard_map/ppermute | solution.py:189
  60.6 9.4 %collective-permute-start.10 = (bf16[4,64,512]{2,1,0:T(8,128)(2,1)S(1)}, bf16[4,64,512]{2,1,0:T(8,128)(2,1)S(1)}, u32[]{:S(2)}, u32[]{:S(2)}) collective-permute-start(bf16[4,64,512]{2,1,0:T(8,128)(2,1)S(1)} %get-tuple-element.38), channel_id=1, source_target_pairs={{0,48},{1,49},{2,50},{3,51},{8,11},{9,8},{10,9},{11,10},{16,0},{17... | collective-permute-start | bytes 786440 | tf_op jit(solution)/shard_map/ppermute | solution.py:189
  63.2 11.1 %collective-permute-start.12 = (bf16[4,64,512]{2,1,0:T(8,128)(2,1)S(1)}, bf16[4,64,512]{2,1,0:T(8,128)(2,1)S(1)}, u32[]{:S(2)}, u32[]{:S(2)}) collective-permute-start(bf16[4,64,512]{2,1,0:T(8,128)(2,1)S(1)} %get-tuple-element.40), channel_id=1, source_target_pairs={{0,16},{1,17},{2,18},{3,19},{8,9},{9,10},{10,11},{11,8},{16,32},{1... | collective-permute-start | bytes 786440 | tf_op jit(solution)/shard_map/ppermute | solution.py:189
  63.9 10.4 %collective-permute-start.13 = (bf16[4,64,512]{2,1,0:T(8,128)(2,1)S(1)}, bf16[4,64,512]{2,1,0:T(8,128)(2,1)S(1)}, u32[]{:S(2)}, u32[]{:S(2)}) collective-permute-start(bf16[4,64,512]{2,1,0:T(8,128)(2,1)S(1)} %get-tuple-element.41), channel_id=1, source_target_pairs={{0,32},{1,33},{2,34},{3,35},{8,10},{9,11},{10,8},{11,9},{16,48},{1... | collective-permute-start | bytes 786440 | tf_op jit(solution)/shard_map/ppermute | solution.py:189
  68.7 6.3 %collective-permute-start.14 = (bf16[4,64,512]{2,1,0:T(8,128)(2,1)S(1)}, bf16[4,64,512]{2,1,0:T(8,128)(2,1)S(1)}, u32[]{:S(2)}, u32[]{:S(2)}) collective-permute-start(bf16[4,64,512]{2,1,0:T(8,128)(2,1)S(1)} %get-tuple-element.42), channel_id=1, source_target_pairs={{0,48},{1,49},{2,50},{3,51},{8,11},{9,8},{10,9},{11,10},{16,0},{17... | collective-permute-start | bytes 786440 | tf_op jit(solution)/shard_map/ppermute | solution.py:189
  75.2 6.8 %collective-permute-start.15 = (bf16[128,512]{1,0:T(8,128)(2,1)S(1)}, bf16[128,512]{1,0:T(8,128)(2,1)S(1)}, u32[]{:S(2)}, u32[]{:S(2)}) collective-permute-start(bf16[128,512]{1,0:T(8,128)(2,1)S(1)} %get-tuple-element.44), channel_id=1, source_target_pairs={{0,1},{1,2},{2,3},{3,0},{8,24},{9,25},{10,26},{11,27},{16,17},{17,... | collective-permute-start | bytes 393224 | tf_op jit(solution)/shard_map/ppermute | solution.py:189
  75.3 6.7 %collective-permute-start.16 = (bf16[128,512]{1,0:T(8,128)(2,1)S(1)}, bf16[128,512]{1,0:T(8,128)(2,1)S(1)}, u32[]{:S(2)}, u32[]{:S(2)}) collective-permute-start(bf16[128,512]{1,0:T(8,128)(2,1)S(1)} %get-tuple-element.45), channel_id=1, source_target_pairs={{0,2},{1,3},{2,0},{3,1},{8,40},{9,41},{10,42},{11,43},{16,18},{17,... | collective-permute-start | bytes 393224 | tf_op jit(solution)/shard_map/ppermute | solution.py:189
  76.8 5.8 %collective-permute-start.17 = (bf16[128,512]{1,0:T(8,128)(2,1)S(1)}, bf16[128,512]{1,0:T(8,128)(2,1)S(1)}, u32[]{:S(2)}, u32[]{:S(2)}) collective-permute-start(bf16[128,512]{1,0:T(8,128)(2,1)S(1)} %get-tuple-element.46), channel_id=1, source_target_pairs={{0,3},{1,0},{2,1},{3,2},{8,56},{9,57},{10,58},{11,59},{16,19},{17,... | collective-permute-start | bytes 393224 | tf_op jit(solution)/shard_map/ppermute | solution.py:189
  82.7 3.4 %collective-permute-start.18 = (bf16[4,16,512]{2,1,0:T(8,128)(2,1)S(1)}, bf16[4,16,512]{2,1,0:T(8,128)(2,1)S(1)}, u32[]{:S(2)}, u32[]{:S(2)}) collective-permute-start(bf16[4,16,512]{2,1,0:T(8,128)(2,1)S(1)} %get-tuple-element.48), channel_id=1, source_target_pairs={{0,8},{8,0},{1,9},{9,1},{2,10},{10,2},{3,11},{11,3},{4,12},{12,4},... | collective-permute-start | bytes 196616 | tf_op jit(solution)/shard_map/ppermute | solution.py:175
